TPU v7x, 512 devices: a whole 4x4x16 slice. The times are simulated.
512 devices in a mesh: replica: 8 (over y, x_lo), mp: 64 (over z, x_hi, core).
Axes of the slice: x: 4 (x_hi: 2, x_lo: 2; x = x_hi * 2 + x_lo), y: 4, z: 16, core: 2. Of those that a mesh axis runs over, the one named last changes fastest.
Arguments:
- owner_shard: int32 [1024, 256], P(('replica', 'mp')), may hold values from 0 to 63, as said below
- slot_index: int32 [1024, 256], P(('replica', 'mp')), may hold values from 0 to 127
- lengths: int32 [1024], P(('replica', 'mp')), may hold values from 32 to 256
- labels: float32 [1024, 256], P(('replica', 'mp')), may hold values from 0 to 1
- embed_table: bfloat16 [131072, 256], P('mp'), may hold values from -3 to 3
- accumulator: float32 [131072], P('mp'), may hold values from 0.1 to 10
- touched: int32 [8192], P('mp'), may hold values from 0 to 2047, as said below
- w_in: bfloat16 [256, 1024], replicated, may hold values from -0.375 to 0.375
- w_mid: bfloat16 [1024, 1024], replicated, may hold values from -0.1875 to 0.1875
- norm_gain: float32 [1024], replicated, may hold values from 0.5 to 2
- w_out: float32 [1024], replicated, may hold values from -0.1875 to 0.1875
Outputs:
- table_out: bfloat16 [131072, 256], P('mp')
- accum_out: float32 [131072], P('mp')
Inputs may be any that keep to these rules, and one draw needn't show every extreme that they name: `owner_shard`: among the events of one device, every shard is named at most 16 times, and one shard, the same for all devices, is named exactly 16 times by every device. `touched`: the 128 entries of each shard are distinct rows of that shard.
All inputs are finite; a program needn't handle non-finite values.
Results may differ from a plain program's by a relative error of at most 0.0034.
Values may be sent and summed in bfloat16 or wider, within the bound.
A program may use at most 64 MiB of HBM per device.

v0:
```python
import jax
import jax.numpy as jnp
from jax import lax
from jax.sharding import PartitionSpec as P

learn_rate = 1.0


def silu_slope(values):
    sigma_val = jax.nn.sigmoid(values)
    return sigma_val * (1.0 + values * (1.0 - sigma_val))


def encoder_grad(looked_up, labels, live_mask, w_in, w_mid, norm_gain, w_out):
    pre_act = jnp.dot(looked_up, w_in, preferred_element_type=jnp.float32)
    hidden = jax.nn.silu(pre_act)
    inv_rms = lax.rsqrt(jnp.mean(hidden * hidden, axis=-1, keepdims=True) + 1e-06)
    normed = (hidden * inv_rms * norm_gain).astype(jnp.bfloat16)
    mixed = jnp.dot(normed, w_mid, preferred_element_type=jnp.float32)
    output = hidden + jax.nn.silu(mixed)
    logits = jnp.sum(output * w_out, axis=-1)
    d_logit = (jax.nn.sigmoid(logits) - labels) * live_mask
    d_output = d_logit[:, None] * w_out
    d_mixed = (d_output * silu_slope(mixed)).astype(jnp.bfloat16)
    d_normed = jnp.dot(d_mixed, w_mid.T, preferred_element_type=jnp.float32)
    gained = d_normed * norm_gain
    d_hidden = (
        d_output
        + inv_rms * gained
        - hidden * inv_rms**3 * jnp.mean(hidden * gained, axis=-1, keepdims=True)
    )
    d_pre = (d_hidden * silu_slope(pre_act)).astype(jnp.bfloat16)
    return jnp.dot(d_pre, w_in.T, preferred_element_type=jnp.float32).astype(jnp.bfloat16)


def adagrad_rows(grad_rows_in, old_rows, old_acc):
    acc_new = old_acc + jnp.sum(grad_rows_in * grad_rows_in, axis=1)
    new_rows = (
        old_rows.astype(jnp.float32) - learn_rate * grad_rows_in * lax.rsqrt(acc_new)[:, None]
    )
    return (new_rows, acc_new)


def on_device(
    owner_shard,
    slot_index,
    lengths,
    labels,
    embed_table,
    accumulator,
    touched,
    w_in,
    w_mid,
    norm_gain,
    w_out,
):
    mp_count = lax.axis_size("mp")
    samples, length = owner_shard.shape
    events = samples * length
    capacity = max(2, 2 * events // mp_count)
    emb_width = embed_table.shape[1]
    touch_count = touched.shape[0]
    owners = owner_shard.reshape(events)
    slots = slot_index.reshape(events)
    live_mask = (
        (jnp.arange(length, dtype=jnp.int32)[None, :] < lengths[:, None])
        .astype(jnp.float32)
        .reshape(events)
    )
    local_block = embed_table[touched]
    owner_onehot = (owners[:, None] == jnp.arange(mp_count, dtype=jnp.int32)[None, :]).astype(
        jnp.int32
    )
    slot_rank = jnp.sum((jnp.cumsum(owner_onehot, axis=0) - 1) * owner_onehot, axis=1)
    send_pos = owners * capacity + slot_rank
    requests = (
        jnp.full((mp_count * capacity,), -1, jnp.int32)
        .at[send_pos]
        .set(slots)
        .reshape(mp_count, capacity)
    )
    every_block = lax.all_gather(local_block, "mp", axis=0, tiled=True)
    looked_up = every_block[owners * touch_count + slots]
    asked_slots = lax.all_to_all(requests, "mp", split_axis=0, concat_axis=0, tiled=True)
    block_rows = min(events, 512)
    block_count = events // block_rows

    def one_block(pieces):
        return encoder_grad(pieces[0], pieces[1], pieces[2], w_in, w_mid, norm_gain, w_out)

    event_grads = lax.map(
        one_block,
        (
            looked_up.reshape(block_count, block_rows, emb_width),
            labels.reshape(block_count, block_rows),
            live_mask.reshape(block_count, block_rows),
        ),
    ).reshape(events, emb_width)
    outgoing = (
        jnp.zeros((mp_count * capacity, emb_width), jnp.bfloat16)
        .at[send_pos]
        .set(event_grads)
        .reshape(mp_count, capacity, emb_width)
    )
    incoming = lax.all_to_all(outgoing, "mp", split_axis=0, concat_axis=0, tiled=True)
    slot_onehot = (
        asked_slots.reshape(-1)[:, None] == jnp.arange(touch_count, dtype=jnp.int32)[None, :]
    ).astype(jnp.bfloat16)
    grad_block = jnp.einsum(
        "rt,re->te",
        slot_onehot,
        incoming.reshape(-1, emb_width),
        preferred_element_type=jnp.float32,
    )
    touched_acc = accumulator[touched]
    grad_total = lax.psum(grad_block, "replica")
    new_rows, new_acc = adagrad_rows(grad_total, local_block, touched_acc)
    table_out = embed_table.at[touched].set(new_rows.astype(jnp.bfloat16))
    accum_out = accumulator.at[touched].set(new_acc)
    return (table_out, accum_out)


def solution(mesh):
    in_specs = (
        P(("replica", "mp"), None),
        P(("replica", "mp"), None),
        P(("replica", "mp")),
        P(("replica", "mp"), None),
        P("mp", None),
        P("mp"),
        P("mp"),
        P(),
        P(),
        P(),
        P(),
    )
    out_specs = (P("mp", None), P("mp"))
    return jax.shard_map(
        on_device, mesh=mesh, in_specs=in_specs, out_specs=out_specs, check_vma=False
    )
```

profile of v0, /device:TPU:1, one launch (start us, length us, event | category | flops | bytes accessed | tf_op | source)
XLA Modules:
  0.0 316.2 jit_solution(12716276199991593378)
XLA Ops:
  7.2 0.0 copy-start
  7.2 0.0 copy-start.4
  7.2 0.0 copy-start.6
  7.2 0.0 copy-start.12
  7.2 0.0 copy-start.7
  7.2 0.0 copy-start.5
  7.2 0.0 copy-start.11
  7.2 0.0 all-gather.3.cloned.1.call-start
  7.3 1.4 copy.28
  8.6 0.0 copy-done.5
  8.6 0.0 copy-done.11
  8.7 1.5 gather_fusion
  10.1 0.0 all-gather.3.cloned.1.call-update
  10.3 1.2 reduce-window.6
  11.5 0.2 slice_reduce_fusion
  11.7 0.1 fusion.19
  11.9 2.4 scatter_custom_fusion
  14.3 0.7 all_to_all.9
  15.0 19.6 %all-to-all-start = ((s32[64,1,16]{2,1,0:T(1,128)}), s32[64,1,16]{2,1,0:T(1,128)S(1)}, u32[]{:S(2)}, u32[]{:S(2)}) async-start(s32[64,1,16]{2,1,0:T(1,128)} %bitcast.3), calls=%async_computation | async-start | bytes 65536 | tf_op jit(solution)/shard_map/all_to_all | solution.py:84
  34.6 0.1 iota_compare_fusion.4
  34.8 133.3 %all-gather.3.cloned.1.call-done = bf16[8192,256]{1,0:T(8,128)(2,1)} async-done(((bf16[128,256]{1,0:T(8,128)(2,1)}), bf16[8192,256]{1,0:T(8,128)(2,1)}) %all-gather.3.cloned.1.call-update) | async-done | bytes 4194320 | tf_op jit(solution)/shard_map/all_gather | solution.py:82
  168.0 4.3 %gather_fusion.1 = bf16[512,256]{1,0:T(8,128)(2,1)S(1)} fusion(bf16[8192,256]{1,0:T(8,128)(2,1)} %all-gather.3.cloned.1.call-done, s32[1024]{0:T(1024)S(1)} %pad_clamp_fusion), kind=kCustom, calls=%fused_computation.1 | custom fusion | bytes 526336 | tf_op jit(solution)/shard_map/gather | solution.py:83
  172.3 0.0 copy-start.9
  172.3 0.0 copy-start.10
  172.3 1.9 multiply_reduce_fusion.2
  174.2 2.3 multiply_reduce_fusion.1
  176.6 0.0 copy-start.8
  176.6 2.0 multiply_reduce_fusion
  178.6 2.4 convolution_convert_fusion
  181.0 3.5 %scatter_custom_fusion.1 = bf16[1024,256]{1,0:T(8,128)(2,1)} fusion(s32[512]{0:T(512)S(1)} %bitcast.53, bf16[512,256]{1,0:T(8,128)(2,1)} %convolution_convert_fusion, bf16[]{:T(256)} %constant.35.clone.1), kind=kCustom, calls=%fused_computation.30 | custom fusion | bytes 524800 | tf_op jit(solution)/shard_map/scatter | solution.py:102
  184.5 0.0 all-to-all-done
  184.6 8.1 %all-to-all-start.1 = ((bf16[64,16,256]{2,1,0:T(8,128)(2,1)}), bf16[64,16,256]{2,1,0:T(8,128)(2,1)}, u32[]{:S(2)}, u32[]{:S(2)}) async-start(bf16[64,16,256]{2,1,0:T(8,128)(2,1)} %bitcast.43), calls=%async_computation.1 | async-start | bytes 1048576 | tf_op jit(solution)/shard_map/all_to_all | solution.py:105
  192.7 0.0 all-reduce.2.cloned.1.call-start
  192.7 0.5 broadcast.180
  193.2 0.7 reduce.5
  194.0 0.1 eq.48
  194.0 32.5 %all-to-all-done.1 = bf16[64,16,256]{2,1,0:T(8,128)(2,1)} async-done(((bf16[64,16,256]{2,1,0:T(8,128)(2,1)}), bf16[64,16,256]{2,1,0:T(8,128)(2,1)}, u32[]{:S(2)}, u32[]{:S(2)}) %all-to-all-start.1) | async-done | bytes 524320 | tf_op jit(solution)/shard_map/all_to_all | solution.py:105
  226.5 2.2 fusion.14
  228.7 0.0 all-reduce.2.cloned.1.call-update
  228.7 1.1 gather_fusion.2
  229.9 74.4 %all-reduce.2.cloned.1.call-done = f32[128,256]{1,0:T(8,128)} async-done(((f32[128,256]{1,0:T(8,128)}), f32[128,256]{1,0:T(8,128)}) %all-reduce.2.cloned.1.call-update) | async-done | bytes 131088 | tf_op jit(solution)/shard_map/psum | solution.py:116
  304.3 1.0 multiply_reduce_fusion.3
  305.3 1.0 scatter_fusion
  306.3 0.0 copy-start.1
  306.3 0.0 copy-done.3
  306.3 2.1 scatter_custom_fusion.2
  308.4 0.0 copy-start.2
  308.4 1.0 copy-done.2
  (31 shorter events, 0.2 us)
Async XLA Ops:
  7.2 167.1 %copy-start = (bf16[1024,1024]{1,0:T(8,128)(2,1)S(1)}, bf16[1024,1024]{1,0:T(8,128)(2,1)}, u32[]{:S(2)}) copy-start(bf16[1024,1024]{1,0:T(8,128)(2,1)} %param.19) | copy-start | bytes 6291460
  7.2 3.0 copy-start.4
  7.2 3.0 copy-start.6
  7.2 27.4 %copy-start.12 = (s32[2]{0:T(128)S(1)}, s32[2]{0:T(128)}, u32[]{:S(2)}) copy-start(s32[2]{0:T(128)} %param.13) | copy-start | bytes 28
  7.2 27.5 %copy-start.7 = (f32[2,256]{1,0:T(2,128)S(1)}, f32[2,256]{1,0:T(2,128)}, u32[]{:S(2)}) copy-start(f32[2,256]{1,0:T(2,128)} %param.14) | copy-start | bytes 6148
  7.2 1.4 copy-start.5
  7.2 1.4 copy-start.11
  7.2 160.8 %all-gather.3.cloned.1.call-start = ((), (), s32[]{:S(2)}) async-start(), calls=%async_computation.3 | async-start | bytes 4259840 | tf_op jit(solution)/shard_map/all_gather | solution.py:82
  15.0 169.5 %all-to-all-start = ((s32[64,1,16]{2,1,0:T(1,128)}), s32[64,1,16]{2,1,0:T(1,128)S(1)}, u32[]{:S(2)}, u32[]{:S(2)}) async-start(s32[64,1,16]{2,1,0:T(1,128)} %bitcast.3), calls=%async_computation | async-start | bytes 65536 | tf_op jit(solution)/shard_map/all_to_all | solution.py:84
  172.3 1.9 copy-start.9
  172.3 1.9 copy-start.10
  176.6 2.0 copy-start.8
  181.0 125.3 %copy-start.3 = (bf16[128,256]{1,0:T(8,128)(2,1)S(1)}, bf16[128,256]{1,0:T(8,128)(2,1)}, u32[]{:S(2)}) copy-start(bf16[128,256]{1,0:T(8,128)(2,1)} %gather_fusion) | copy-start | bytes 196612
  184.6 42.0 %all-to-all-start.1 = ((bf16[64,16,256]{2,1,0:T(8,128)(2,1)}), bf16[64,16,256]{2,1,0:T(8,128)(2,1)}, u32[]{:S(2)}, u32[]{:S(2)}) async-start(bf16[64,16,256]{2,1,0:T(8,128)(2,1)} %bitcast.43), calls=%async_computation.1 | async-start | bytes 1048576 | tf_op jit(solution)/shard_map/all_to_all | solution.py:105
  192.7 111.6 %all-reduce.2.cloned.1.call-start = ((), (), s32[]{:S(2)}) async-start(), calls=%async_computation.2 | async-start | bytes 262144 | tf_op jit(solution)/shard_map/psum | solution.py:116
  306.3 2.1 copy-start.1
  308.4 1.0 copy-start.2
Sparse Core Ops, SparseCore 0:
  11.3 156.6 all-gather.2
  228.8 75.3 all-reduce.1
where the time goes:
time: 321 us; the launch traced here: 316 us
  waiting for transfers between devices  240 us (75%)
  starting transfers between devices  27.8 us (9%)
  local copies, waits for them, and re-layouts  17.8 us (6%)
  between operations  14.4 us (4%)
  matrix products  10.8 us (3%)
  other arithmetic  5.35 us (2%)
    all_gather x1, waiting for transfers between devices, on_device(): every_block = lax.all_gather(local_block, 'mp', axis=0, tiled=True)  133 us
    psum x1, waiting for transfers between devices, on_device(): grad_total = lax.psum(grad_block, 'replica')  74.4 us
    all_to_all x1, waiting for transfers between devices, on_device(): lax.all_to_all(outgoing, 'mp', split_axis=0, concat_axis=0, tiled=True)  32.5 us
    all_to_all x1, starting transfers between devices, on_device(): lax.all_to_all(requests, 'mp', split_axis=0, concat_axis=0, tiled=True)  19.6 us
    all_to_all x1, starting transfers between devices, on_device(): lax.all_to_all(outgoing, 'mp', split_axis=0, concat_axis=0, tiled=True)  8.11 us
  transfers between devices with their start and end apart: 4, of which 3 were waited for; matrix products, arithmetic and copies ran while one was open for 7% of the time, Pallas kernels for 0%

commit v1 on v0

v1 whole, which is shorter than its diff:
```python
import functools

import jax
import jax.numpy as jnp
from jax import lax
from jax.experimental import pallas as pl
from jax.experimental.pallas import tpu as pltpu
from jax.sharding import PartitionSpec as P

MESH = pl.DeviceIdType.MESH
F32 = jnp.float32
BF16 = jnp.bfloat16
learn_rate = 1.0

N_CORE = 2
N_XHI = 2


def split3(values):
    high = values.astype(BF16)
    rest = values - high.astype(F32)
    mid = rest.astype(BF16)
    low = (rest - mid.astype(F32)).astype(BF16)
    return high, mid, low


def dot_nn(a, b):
    return jnp.dot(a, b, preferred_element_type=F32)


def dot_nt(a, b):
    return lax.dot_general(a, b, (((1,), (1,)), ((), ())), preferred_element_type=F32)


def silu_slope(values, sigma_val):
    return sigma_val * (1.0 + values * (1.0 - sigma_val))


def iota(shape, dim):
    return lax.broadcasted_iota(jnp.int32, shape, dim)


def reduce_kernel(
    n_rep,
    n_z,
    owner_hbm,
    slot_hbm,
    len_ref,
    label_hbm,
    table_hbm,
    acc_hbm,
    touched_hbm,
    w_in_hbm,
    w_mid_hbm,
    gain_hbm,
    w_out_hbm,
    rows_ref,
    acc_out_ref,
    owner_v,
    slot_v,
    label_v,
    table_v,
    acc_v,
    touched_v,
    w_in_v,
    w_mid_v,
    gain_v,
    w_out_v,
    in_sem,
    hist,
    core_recv,
    z_send,
    z_recv,
    p_send,
    p_recv,
    core_sem,
    z_sem,
    p_sem,
):
    rep = lax.axis_index("replica")
    mp = lax.axis_index("mp")
    core = lax.rem(mp, N_CORE)
    x_hi = lax.rem(lax.div(mp, N_CORE), N_XHI)
    z = lax.div(mp, N_CORE * N_XHI)

    def mp_of(z_i, x_i, core_i):
        return (z_i * N_XHI + x_i) * N_CORE + core_i

    z_shift = sorted(range(1, n_z), key=lambda s: -min(s, n_z - s))
    z_peers = [lax.rem(z + s, n_z) for s in z_shift]
    p_shift = [(r, x) for r in range(n_rep) for x in range(N_XHI) if (r, x) != (0, 0)]
    p_peers = [(lax.rem(rep + r, n_rep), lax.rem(x_hi + x, N_XHI)) for r, x in p_shift]
    partner = mp_of(z, x_hi, 1 - core)

    barrier = pltpu.get_barrier_semaphore()
    for z_i in z_peers:
        pl.semaphore_signal(
            barrier, inc=1, device_id=(rep, mp_of(z_i, x_hi, core)), device_id_type=MESH
        )
    for rep_i, x_i in p_peers:
        pl.semaphore_signal(
            barrier, inc=1, device_id=(rep_i, mp_of(z, x_i, core)), device_id_type=MESH
        )
    pl.semaphore_signal(barrier, inc=1, device_id=(rep, partner), device_id_type=MESH)

    sources = [
        (owner_hbm, owner_v),
        (slot_hbm, slot_v),
        (label_hbm, label_v),
        (touched_hbm, touched_v),
        (acc_hbm, acc_v),
        (gain_hbm, gain_v),
        (w_out_hbm, w_out_v),
        (table_hbm, table_v),
        (w_in_hbm, w_in_v),
        (w_mid_hbm, w_mid_v),
    ]
    loads = [
        pltpu.make_async_copy(src, dst, in_sem.at[i]) for i, (src, dst) in enumerate(sources)
    ]
    for load in loads:
        load.start()
    for load in loads[:3]:
        load.wait()

    samples, length = owner_v.shape
    events = samples * length
    n_rows = hist.shape[0]
    slots_n = hist.shape[1]
    half = n_rows // 2
    row = iota((n_rows, events), 0)
    kind = lax.rem(row, 2)
    row_x = lax.rem(lax.div(row, 2), N_XHI)
    row_z = lax.rem(lax.div(row, 2 * N_XHI), n_z)
    row_core = lax.div(row, half)
    row_owner = mp_of(row_z, row_x, row_core)

    def flat(ref):
        return jnp.concatenate([ref[s : s + 1, :] for s in range(samples)], axis=1)

    live = jnp.concatenate(
        [(iota((1, length), 1) < len_ref[s]).astype(F32) for s in range(samples)], axis=1
    )
    high, mid, low = (part.astype(F32) for part in split3(flat(label_v)))
    hit = row_owner == flat(owner_v)
    counted = hit & (kind == 0)
    labelled = hit & (kind == 1)
    zero = jnp.zeros((n_rows, events), F32)
    lhs = jnp.concatenate(
        [
            jnp.where(counted, live, jnp.where(labelled, live * high, zero)).astype(BF16),
            jnp.where(labelled, live * mid, zero).astype(BF16),
            jnp.where(labelled, live * low, zero).astype(BF16),
        ],
        axis=1,
    )
    slot_hot = (iota((slots_n, events), 0) == flat(slot_v)).astype(F32).astype(BF16)
    hist[...] = dot_nt(lhs, jnp.concatenate([slot_hot] * 3, axis=1))

    pl.semaphore_wait(barrier, len(z_peers) + len(p_peers) + 1)

    core_copy = pltpu.make_async_remote_copy(
        src_ref=hist.at[pl.ds(pl.multiple_of((1 - core) * half, half), half)],
        dst_ref=core_recv,
        send_sem=core_sem.at[0],
        recv_sem=core_sem.at[1],
        device_id=(rep, partner),
        device_id_type=MESH,
    )
    core_copy.start()

    for load in loads[3:]:
        load.wait()
    rows_n = table_v.shape[0]
    lanes = acc_v.shape[1]
    touched_row = touched_v[...]
    eye = iota((slots_n, slots_n), 0) == iota((slots_n, slots_n), 1)

    def to_column(line):
        return jnp.sum(jnp.where(eye, line, 0.0), axis=1, keepdims=True)

    core_copy.wait_recv()
    own = hist[pl.ds(pl.multiple_of(core * half, half), half), :] + core_recv[...]
    part = half // n_z
    for z_i in range(n_z):
        z_send[z_i] = own[z_i * part : (z_i + 1) * part, :]
    for i, z_i in enumerate(z_peers):
        pltpu.make_async_remote_copy(
            src_ref=z_send.at[z_i],
            dst_ref=z_recv.at[z],
            send_sem=z_sem.at[0],
            recv_sem=z_sem.at[1],
            device_id=(rep, mp_of(z_i, x_hi, core)),
            device_id_type=MESH,
        ).start()
    z_recv[z] = z_send[z]

    touched_col = to_column(touched_row.astype(F32)).astype(jnp.int32)
    pick = (iota((slots_n, rows_n), 1) == touched_col).astype(F32).astype(BF16)
    old_rows = dot_nn(pick, table_v[...])
    gain = gain_v[...]
    w_out = w_out_v[...]
    width = w_out.shape[1]
    pre_act = dot_nn(old_rows.astype(BF16), w_in_v[...])
    sig_pre = jax.nn.sigmoid(pre_act)
    hidden = pre_act * sig_pre
    inv_rms = lax.rsqrt(jnp.sum(hidden * hidden, axis=1, keepdims=True) * (1.0 / width) + 1e-06)
    mixed = dot_nn((hidden * inv_rms * gain).astype(BF16), w_mid_v[...])
    sig_mix = jax.nn.sigmoid(mixed)
    logits = jnp.sum((hidden + mixed * sig_mix) * w_out, axis=1, keepdims=True)
    click = jax.nn.sigmoid(logits)
    d_mixed = (w_out * silu_slope(mixed, sig_mix)).astype(BF16)
    gained = dot_nt(d_mixed, w_mid_v[...]) * gain
    dotted = jnp.sum(hidden * gained, axis=1, keepdims=True) * (1.0 / width)
    d_hidden = w_out + inv_rms * gained - hidden * (inv_rms * inv_rms * inv_rms * dotted)
    d_pre = (d_hidden * silu_slope(pre_act, sig_pre)).astype(BF16)
    unit_grad = dot_nt(d_pre, w_in_v[...])

    lo_col = lax.rem(touched_col, lanes)
    hi_col = lax.div(touched_col, lanes)
    acc_rows = acc_v.shape[0]
    hi_hot = (iota((slots_n, acc_rows), 1) == hi_col).astype(F32).astype(BF16)
    lo_hit = iota((slots_n, lanes), 1) == lo_col
    acc_parts = [dot_nn(hi_hot, piece) for piece in split3(acc_v[...])]
    acc_lines = acc_parts[0] + acc_parts[1] + acc_parts[2]
    old_acc = jnp.sum(jnp.where(lo_hit, acc_lines, 0.0), axis=1, keepdims=True)
    hi_hot_t = (
        (iota((acc_rows, slots_n), 0) == lax.div(touched_row, lanes)).astype(F32).astype(BF16)
    )
    acc_hit = dot_nn(hi_hot_t, lo_hit.astype(F32).astype(BF16)) > 0.5

    pltpu.make_async_copy(
        z_recv.at[pl.ds(0, n_z - 1)], z_recv.at[pl.ds(0, n_z - 1)], z_sem.at[1]
    ).wait()
    column = z_recv[0]
    for z_i in range(1, n_z):
        column = column + z_recv[z_i]
    for x_i in range(N_XHI):
        p_send[x_i] = column[x_i * 2 : x_i * 2 + 2, :]
    mine = x_hi * n_rep + rep
    for i, (rep_i, x_i) in enumerate(p_peers):
        pltpu.make_async_remote_copy(
            src_ref=p_send.at[x_i],
            dst_ref=p_recv.at[mine],
            send_sem=p_sem.at[0],
            recv_sem=p_sem.at[1],
            device_id=(rep_i, mp_of(z, x_i, core)),
            device_id_type=MESH,
        ).start()
    p_recv[mine] = p_send[x_hi]
    n_p = len(p_peers)
    pltpu.make_async_copy(
        p_recv.at[pl.ds(0, n_p)], p_recv.at[pl.ds(0, n_p)], p_sem.at[1]
    ).wait()
    total = p_recv[0]
    for i in range(1, n_p + 1):
        total = total + p_recv[i]

    d_sum = to_column(total[0:1, :]) * click - to_column(total[1:2, :])
    grad = d_sum * unit_grad
    acc_new = old_acc + jnp.sum(grad * grad, axis=1, keepdims=True)
    rows_ref[...] = (old_rows - learn_rate * grad * lax.rsqrt(acc_new)).astype(BF16)
    spread = jnp.where(lo_hit, acc_new, 0.0)
    placed = [dot_nn(hi_hot_t, piece) for piece in split3(spread)]
    acc_out_ref[...] = jnp.where(acc_hit, placed[0] + placed[1] + placed[2], acc_v[...])

    core_copy.wait_send()
    pltpu.make_async_copy(
        z_send.at[pl.ds(0, n_z - 1)], z_send.at[pl.ds(0, n_z - 1)], z_sem.at[0]
    ).wait()
    pltpu.make_async_copy(
        p_recv.at[pl.ds(0, n_p)], p_recv.at[pl.ds(0, n_p)], p_sem.at[0]
    ).wait()


def scatter_kernel(touched_ref, rows_ref, acc_ref, table_ref, table_out_ref, acc_out_ref):
    rows_n, slots_n = table_ref.shape[0], touched_ref.shape[1]
    place = (iota((rows_n, slots_n), 0) == touched_ref[...]).astype(F32)
    hit = jnp.sum(place, axis=1, keepdims=True) > 0.5
    placed = dot_nn(place.astype(BF16), rows_ref[...])
    table_out_ref[...] = jnp.where(hit, placed, table_ref[...].astype(F32)).astype(BF16)
    acc_out_ref[...] = acc_ref[...]


def on_device(
    n_rep,
    n_z,
    owner_shard,
    slot_index,
    lengths,
    labels,
    embed_table,
    accumulator,
    touched,
    w_in,
    w_mid,
    norm_gain,
    w_out,
):
    rows_n, emb = embed_table.shape
    slots_n = touched.shape[0]
    width = w_out.shape[0]
    lanes = 128
    acc2 = accumulator.reshape(rows_n // lanes, lanes)
    touched2 = touched.reshape(1, slots_n)
    any_spec = pl.BlockSpec(memory_space=pl.ANY)
    vmem = pl.BlockSpec(memory_space=pltpu.VMEM)
    smem = pl.BlockSpec(memory_space=pltpu.SMEM)
    n_rows = n_z * N_XHI * N_CORE * 2
    part = n_rows // 2 // n_z
    new_rows, acc_new = pl.pallas_call(
        functools.partial(reduce_kernel, n_rep, n_z),
        out_shape=(
            jax.ShapeDtypeStruct((slots_n, emb), BF16),
            jax.ShapeDtypeStruct(acc2.shape, F32),
        ),
        in_specs=[any_spec, any_spec, smem] + [any_spec] * 8,
        out_specs=(vmem, vmem),
        scratch_shapes=[
            pltpu.VMEM(owner_shard.shape, jnp.int32),
            pltpu.VMEM(slot_index.shape, jnp.int32),
            pltpu.VMEM(labels.shape, F32),
            pltpu.VMEM(embed_table.shape, BF16),
            pltpu.VMEM(acc2.shape, F32),
            pltpu.VMEM(touched2.shape, jnp.int32),
            pltpu.VMEM(w_in.shape, BF16),
            pltpu.VMEM(w_mid.shape, BF16),
            pltpu.VMEM((1, width), F32),
            pltpu.VMEM((1, width), F32),
            pltpu.SemaphoreType.DMA((10,)),
            pltpu.VMEM((n_rows, slots_n), F32),
            pltpu.VMEM((n_rows // 2, slots_n), F32),
            pltpu.VMEM((n_z, part, slots_n), F32),
            pltpu.VMEM((n_z, part, slots_n), F32),
            pltpu.VMEM((N_XHI, 2, slots_n), F32),
            pltpu.VMEM((N_XHI * n_rep, 2, slots_n), F32),
            pltpu.SemaphoreType.DMA((2,)),
            pltpu.SemaphoreType.DMA((2,)),
            pltpu.SemaphoreType.DMA((2,)),
        ],
        compiler_params=pltpu.CompilerParams(
            collective_id=0, has_side_effects=True, vmem_limit_bytes=32 * 1024 * 1024
        ),
        name="reduce",
    )(
        owner_shard,
        slot_index,
        lengths,
        labels,
        embed_table,
        acc2,
        touched2,
        w_in,
        w_mid,
        norm_gain.reshape(1, width),
        w_out.reshape(1, width),
    )
    table_out, accum_out = pl.pallas_call(
        scatter_kernel,
        out_shape=(
            jax.ShapeDtypeStruct(embed_table.shape, BF16),
            jax.ShapeDtypeStruct(acc2.shape, F32),
        ),
        in_specs=[vmem] * 4,
        out_specs=(vmem, vmem),
        compiler_params=pltpu.CompilerParams(vmem_limit_bytes=24 * 1024 * 1024),
        name="scatter",
    )(touched2, new_rows, acc_new, embed_table)
    return (table_out, accum_out.reshape(rows_n))


def solution(mesh):
    n_rep = mesh.shape["replica"]
    n_z = mesh.shape["mp"] // (N_CORE * N_XHI)
    in_specs = (
        P(("replica", "mp"), None),
        P(("replica", "mp"), None),
        P(("replica", "mp")),
        P(("replica", "mp"), None),
        P("mp", None),
        P("mp"),
        P("mp"),
        P(),
        P(),
        P(),
        P(),
    )
    out_specs = (P("mp", None), P("mp"))
    return jax.shard_map(
        functools.partial(on_device, n_rep, n_z),
        mesh=mesh,
        in_specs=in_specs,
        out_specs=out_specs,
        check_vma=False,
    )
```

time: 321 us -> 41.4 us (0.13); the launches traced: 316 us -> 41 us
  waiting for transfers between devices: 240 us -> 0 us
  Pallas kernels: 0 us -> 31 us
  starting transfers between devices: 27.8 us -> 0 us
  between operations: 14.4 us -> 0.66 us
  matrix products: 10.8 us -> 0 us
  local copies, waits for them, and re-layouts: 17.8 us -> 9.27 us
  other arithmetic: 5.35 us -> 0 us
    all_gather x1 -> x0, waiting for transfers between devices: 133 us -> none  [on_device(): every_block = lax.all_gather(local_block, 'mp', axis=0, tiled=True)]
    psum x1 -> x0, waiting for transfers between devices: 74.4 us -> none  [on_device(): grad_total = lax.psum(grad_block, 'replica')]
    all_to_all x2 -> x0, waiting for transfers between devices: 32.5 us -> none  [the longest x1 32.5 us: on_device(): lax.all_to_all(outgoing, 'mp', split_axis=0, concat_axis=0, tiled=True)]
    pallas_call x0 -> x2, Pallas kernels: none -> 31 us  [the longest x1 29.6 us: on_device(): pl.pallas_call(functools.partial(reduce_kernel, n_rep, n_z), out_shape=(j...]
    all_to_all x2 -> x0, starting transfers between devices: 27.7 us -> none  [the longest x1 19.6 us: on_device(): lax.all_to_all(requests, 'mp', split_axis=0, concat_axis=0, tiled=True)]
    dot_general x5 -> x0, matrix products: 10.8 us -> none  [the longest x1 2.41 us: encoder_grad(): jnp.dot(d_pre, w_in.T, preferred_element_type=jnp.float32)]
    scatter x3 -> x0, local copies, waits for them, and re-layouts: 6.97 us -> none  [the longest x1 3.53 us: on_device(): outgoing = jnp.zeros((mp_count * capacity, emb_width), jnp.bfloat16).at[s...]
    gather x3 -> x0, local copies, waits for them, and re-layouts: 6.92 us -> none  [the longest x1 4.29 us: on_device(): looked_up = every_block[owners * touch_count + slots]]
  transfers between devices with their start and end apart: 4 -> 0, of which waited for: 3 -> 0; matrix products, arithmetic and copies ran while one was open for 7% -> 0% of each run, Pallas kernels for 0% -> 0%
where the time goes in v1:
time: 41.4 us; the launch traced here: 41 us
  Pallas kernels  31 us (75%)
  local copies, waits for them, and re-layouts  9.27 us (22%)
  between operations  0.66 us (2%)
    pallas_call x1, Pallas kernels, on_device(): pl.pallas_call(functools.partial(reduce_kernel, n_rep, n_z), out_shape=(j...  29.6 us
    unnamed x22, local copies, waits for them, and re-layouts  9.27 us
    pallas_call x1, Pallas kernels, on_device(): pl.pallas_call(scatter_kernel, out_shape=(jax.ShapeDtypeStruct(embed_tabl...  1.46 us

profile of v1, /device:TPU:1, one launch (start us, length us, event | category | flops | bytes accessed | tf_op | source)
XLA Modules:
  0.0 41.0 jit_solution(11571949004880691166)
XLA Ops:
  0.6 0.0 copy-start
  0.6 1.2 %copy-done = bf16[2048,256]{1,0:T(8,128)(2,1)S(1)} copy-done((bf16[2048,256]{1,0:T(8,128)(2,1)S(1)}, bf16[2048,256]{1,0:T(8,128)(2,1)}, u32[]{:S(2)}) %copy-start) | copy-done | bytes 1048600
  1.9 0.0 copy-start.1
  1.9 1.6 %copy-done.1 = bf16[1024,1024]{1,0:T(8,128)(2,1)S(1)} copy-done((bf16[1024,1024]{1,0:T(8,128)(2,1)S(1)}, bf16[1024,1024]{1,0:T(8,128)(2,1)}, u32[]{:S(2)}) %copy-start.1) | copy-done | bytes 2097176
  3.5 0.0 copy-start.2
  3.5 1.0 %copy-done.2 = bf16[256,1024]{1,0:T(8,128)(2,1)S(1)} copy-done((bf16[256,1024]{1,0:T(8,128)(2,1)S(1)}, bf16[256,1024]{1,0:T(8,128)(2,1)}, u32[]{:S(2)}) %copy-start.2) | copy-done | bytes 524312
  4.5 0.0 copy-start.3
  4.5 0.7 %copy-done.3 = f32[2048]{0:T(1024)S(1)} copy-done((f32[2048]{0:T(1024)S(1)}, f32[2048]{0:T(1024)}, u32[]{:S(2)}) %copy-start.3) | copy-done | bytes 8216
  5.2 0.0 copy-start.4
  5.2 0.7 %copy-done.4 = f32[1024]{0:T(1024)S(1)} copy-done((f32[1024]{0:T(1024)S(1)}, f32[1024]{0:T(1024)}, u32[]{:S(2)}) %copy-start.4) | copy-done | bytes 4120
  5.9 0.0 copy-start.5
  5.9 0.7 %copy-done.5 = f32[1024]{0:T(1024)S(1)} copy-done((f32[1024]{0:T(1024)S(1)}, f32[1024]{0:T(1024)}, u32[]{:S(2)}) %copy-start.5) | copy-done | bytes 4120
  6.6 0.0 copy-start.6
  6.6 0.7 %copy-done.6 = s32[2,256]{1,0:T(2,128)S(1)} copy-done((s32[2,256]{1,0:T(2,128)S(1)}, s32[2,256]{1,0:T(2,128)}, u32[]{:S(2)}) %copy-start.6) | copy-done | bytes 2072
  7.2 0.0 copy-start.7
  7.2 0.7 %copy-done.7 = s32[2,256]{1,0:T(2,128)S(1)} copy-done((s32[2,256]{1,0:T(2,128)S(1)}, s32[2,256]{1,0:T(2,128)}, u32[]{:S(2)}) %copy-start.7) | copy-done | bytes 2072
  7.9 0.0 copy-start.8
  7.9 0.7 %copy-done.8 = f32[2,256]{1,0:T(2,128)S(1)} copy-done((f32[2,256]{1,0:T(2,128)S(1)}, f32[2,256]{1,0:T(2,128)}, u32[]{:S(2)}) %copy-start.8) | copy-done | bytes 2072
  8.6 0.0 copy-start.9
  8.6 0.7 %copy-done.9 = s32[128]{0:T(128)S(1)} copy-done((s32[128]{0:T(128)S(1)}, s32[128]{0:T(128)}, u32[]{:S(2)}) %copy-start.9) | copy-done | bytes 536
  9.3 0.0 copy-start.10
  9.3 0.7 %copy-done.10 = s32[2]{0:T(128)S(1)} copy-done((s32[2]{0:T(128)S(1)}, s32[2]{0:T(128)}, u32[]{:S(2)}) %copy-start.10) | copy-done | bytes 32
  9.9 29.6 %reduce.1 = (bf16[128,256]{1,0:T(8,128)(2,1)S(1)}, f32[16,128]{1,0:T(8,128)S(1)}) custom-call(s32[2,256]{1,0:T(2,128)S(1)} %copy-done.6, s32[2,256]{1,0:T(2,128)S(1)} %copy-done.7, s32[2]{0:T(128)S(1)} %copy-done.10, f32[2,256]{1,0:T(2,128)S(1)} %copy-done.8, bf16[2048,256]{1,0:T(8,128)(2,1)S(1)} %copy-done, f32[16,128]{1,0:T(8,128)S(1)} %bitcast.5, ...), custom_call_target="tpu_custom_call" | custom-call | tf_op jit(solution)/shard_map/reduce/pallas_call | solution.py:311
  39.5 1.5 %scatter.1 = (bf16[2048,256]{1,0:T(8,128)(2,1)}, f32[16,128]{1,0:T(8,128)}) custom-call(s32[1,128]{1,0:T(1,128)S(1)} %bitcast.9, bf16[128,256]{1,0:T(8,128)(2,1)S(1)} %get-tuple-element.6.rows_ref, f32[16,128]{1,0:T(8,128)S(1)} %get-tuple-element.7.acc_ref, bf16[2048,256]{1,0:T(8,128)(2,1)S(1)} %copy-done), custom_call_target="tpu_custom_call" | custom-call | tf_op jit(solution)/shard_map/scatter/pallas_call | solution.py:358
Async XLA Ops:
  0.6 1.2 %copy-start = (bf16[2048,256]{1,0:T(8,128)(2,1)S(1)}, bf16[2048,256]{1,0:T(8,128)(2,1)}, u32[]{:S(2)}) copy-start(bf16[2048,256]{1,0:T(8,128)(2,1)} %table_ref.1) | copy-start | bytes 3145732
  1.9 1.6 %copy-start.1 = (bf16[1024,1024]{1,0:T(8,128)(2,1)S(1)}, bf16[1024,1024]{1,0:T(8,128)(2,1)}, u32[]{:S(2)}) copy-start(bf16[1024,1024]{1,0:T(8,128)(2,1)} %w_mid_hbm.1) | copy-start | bytes 6291460
  3.5 1.0 %copy-start.2 = (bf16[256,1024]{1,0:T(8,128)(2,1)S(1)}, bf16[256,1024]{1,0:T(8,128)(2,1)}, u32[]{:S(2)}) copy-start(bf16[256,1024]{1,0:T(8,128)(2,1)} %w_in_hbm.1) | copy-start | bytes 1572868
  4.5 0.7 %copy-start.3 = (f32[2048]{0:T(1024)S(1)}, f32[2048]{0:T(1024)}, u32[]{:S(2)}) copy-start(f32[2048]{0:T(1024)} %param.16) | copy-start | bytes 24580
  5.2 0.7 %copy-start.4 = (f32[1024]{0:T(1024)S(1)}, f32[1024]{0:T(1024)}, u32[]{:S(2)}) copy-start(f32[1024]{0:T(1024)} %param.20) | copy-start | bytes 12292
  5.9 0.7 %copy-start.5 = (f32[1024]{0:T(1024)S(1)}, f32[1024]{0:T(1024)}, u32[]{:S(2)}) copy-start(f32[1024]{0:T(1024)} %param.21) | copy-start | bytes 12292
  6.6 0.7 %copy-start.6 = (s32[2,256]{1,0:T(2,128)S(1)}, s32[2,256]{1,0:T(2,128)}, u32[]{:S(2)}) copy-start(s32[2,256]{1,0:T(2,128)} %owner_hbm.1) | copy-start | bytes 6148
  7.2 0.7 %copy-start.7 = (s32[2,256]{1,0:T(2,128)S(1)}, s32[2,256]{1,0:T(2,128)}, u32[]{:S(2)}) copy-start(s32[2,256]{1,0:T(2,128)} %slot_hbm.1) | copy-start | bytes 6148
  7.9 0.7 %copy-start.8 = (f32[2,256]{1,0:T(2,128)S(1)}, f32[2,256]{1,0:T(2,128)}, u32[]{:S(2)}) copy-start(f32[2,256]{1,0:T(2,128)} %label_hbm.1) | copy-start | bytes 6148
  8.6 0.7 %copy-start.9 = (s32[128]{0:T(128)S(1)}, s32[128]{0:T(128)}, u32[]{:S(2)}) copy-start(s32[128]{0:T(128)} %param.17) | copy-start | bytes 1540
  9.3 0.7 %copy-start.10 = (s32[2]{0:T(128)S(1)}, s32[2]{0:T(128)}, u32[]{:S(2)}) copy-start(s32[2]{0:T(128)} %len_ref.1) | copy-start | bytes 28

commit v2 on v1

--- a/solution.py
+++ b/solution.py
@@ -45,7 +45,7 @@
     n_z,
     owner_hbm,
     slot_hbm,
-    len_ref,
+    len_hbm,
     label_hbm,
     table_hbm,
     acc_hbm,
@@ -58,6 +58,7 @@
     acc_out_ref,
     owner_v,
     slot_v,
+    len_s,
     label_v,
     table_v,
     acc_v,
@@ -107,6 +108,7 @@
         (owner_hbm, owner_v),
         (slot_hbm, slot_v),
         (label_hbm, label_v),
+        (len_hbm, len_s),
         (touched_hbm, touched_v),
         (acc_hbm, acc_v),
         (gain_hbm, gain_v),
@@ -120,7 +122,7 @@
     ]
     for load in loads:
         load.start()
-    for load in loads[:3]:
+    for load in loads[:4]:
         load.wait()
 
     samples, length = owner_v.shape
@@ -139,7 +141,7 @@
         return jnp.concatenate([ref[s : s + 1, :] for s in range(samples)], axis=1)
 
     live = jnp.concatenate(
-        [(iota((1, length), 1) < len_ref[s]).astype(F32) for s in range(samples)], axis=1
+        [(iota((1, length), 1) < len_s[s]).astype(F32) for s in range(samples)], axis=1
     )
     high, mid, low = (part.astype(F32) for part in split3(flat(label_v)))
     hit = row_owner == flat(owner_v)
@@ -169,7 +171,7 @@
     )
     core_copy.start()
 
-    for load in loads[3:]:
+    for load in loads[4:]:
         load.wait()
     rows_n = table_v.shape[0]
     lanes = acc_v.shape[1]
@@ -303,22 +305,38 @@
     lanes = 128
     acc2 = accumulator.reshape(rows_n // lanes, lanes)
     touched2 = touched.reshape(1, slots_n)
-    any_spec = pl.BlockSpec(memory_space=pl.ANY)
+    hbm_spec = pl.BlockSpec(memory_space=pltpu.HBM)
     vmem = pl.BlockSpec(memory_space=pltpu.VMEM)
-    smem = pl.BlockSpec(memory_space=pltpu.SMEM)
     n_rows = n_z * N_XHI * N_CORE * 2
     part = n_rows // 2 // n_z
+    operands = [
+        pltpu.with_memory_space_constraint(array, pltpu.HBM)
+        for array in (
+            owner_shard,
+            slot_index,
+            lengths,
+            labels,
+            embed_table,
+            acc2,
+            touched2,
+            w_in,
+            w_mid,
+            norm_gain.reshape(1, width),
+            w_out.reshape(1, width),
+        )
+    ]
     new_rows, acc_new = pl.pallas_call(
         functools.partial(reduce_kernel, n_rep, n_z),
         out_shape=(
             jax.ShapeDtypeStruct((slots_n, emb), BF16),
             jax.ShapeDtypeStruct(acc2.shape, F32),
         ),
-        in_specs=[any_spec, any_spec, smem] + [any_spec] * 8,
+        in_specs=[hbm_spec] * len(operands),
         out_specs=(vmem, vmem),
         scratch_shapes=[
             pltpu.VMEM(owner_shard.shape, jnp.int32),
             pltpu.VMEM(slot_index.shape, jnp.int32),
+            pltpu.SMEM(lengths.shape, jnp.int32),
             pltpu.VMEM(labels.shape, F32),
             pltpu.VMEM(embed_table.shape, BF16),
             pltpu.VMEM(acc2.shape, F32),
@@ -327,7 +345,7 @@
             pltpu.VMEM(w_mid.shape, BF16),
             pltpu.VMEM((1, width), F32),
             pltpu.VMEM((1, width), F32),
-            pltpu.SemaphoreType.DMA((10,)),
+            pltpu.SemaphoreType.DMA((11,)),
             pltpu.VMEM((n_rows, slots_n), F32),
             pltpu.VMEM((n_rows // 2, slots_n), F32),
             pltpu.VMEM((n_z, part, slots_n), F32),
@@ -342,19 +360,7 @@
             collective_id=0, has_side_effects=True, vmem_limit_bytes=32 * 1024 * 1024
         ),
         name="reduce",
-    )(
-        owner_shard,
-        slot_index,
-        lengths,
-        labels,
-        embed_table,
-        acc2,
-        touched2,
-        w_in,
-        w_mid,
-        norm_gain.reshape(1, width),
-        w_out.reshape(1, width),
-    )
+    )(*operands)
     table_out, accum_out = pl.pallas_call(
         scatter_kernel,
         out_shape=(

time: 41.4 us -> 31.5 us (0.76)
  local copies, waits for them, and re-layouts: 9.27 us -> 0.01 us
    unnamed x22 -> x4, local copies, waits for them, and re-layouts: 9.27 us -> 0.01 us
where the time goes in v2:
time: 31.5 us; the launch traced here: 31.3 us
  Pallas kernels  30.7 us (97%)
  between operations  0.67 us (2%)
    pallas_call x1, Pallas kernels, on_device(): pl.pallas_call(functools.partial(reduce_kernel, n_rep, n_z), out_shape=(j...  29.2 us
    pallas_call x1, Pallas kernels, on_device(): pl.pallas_call(scatter_kernel, out_shape=(jax.ShapeDtypeStruct(embed_tabl...  1.47 us

profile of v2, /device:TPU:1, one launch (start us, length us, event | category | flops | bytes accessed | tf_op | source)
XLA Modules:
  0.0 31.3 jit_solution(9752901459152256636)
XLA Ops:
  0.6 0.0 copy-start
  0.6 0.0 copy-start.1
  0.7 29.2 %reduce.1 = (bf16[128,256]{1,0:T(8,128)(2,1)S(1)}, f32[16,128]{1,0:T(8,128)S(1)}) custom-call(s32[2,256]{1,0:T(2,128)} %owner_hbm.1, s32[2,256]{1,0:T(2,128)} %slot_hbm.1, s32[2]{0:T(128)} %len_hbm.1, f32[2,256]{1,0:T(2,128)} %label_hbm.1, bf16[2048,256]{1,0:T(8,128)(2,1)} %table_ref.1, f32[16,128]{1,0:T(8,128)} %bitcast.7, s32[1,128]{1,0:T(1,128)} %bitcast.5, ...), custom_call_target="tpu_custom_call" | custom-call | tf_op jit(solution)/shard_map/reduce/pallas_call | solution.py:328
  29.9 0.0 copy-done
  29.9 0.0 copy-done.1
  29.9 1.5 %scatter.1 = (bf16[2048,256]{1,0:T(8,128)(2,1)}, f32[16,128]{1,0:T(8,128)}) custom-call(s32[1,128]{1,0:T(1,128)S(1)} %bitcast.6, bf16[128,256]{1,0:T(8,128)(2,1)S(1)} %get-tuple-element.6.rows_ref, f32[16,128]{1,0:T(8,128)S(1)} %get-tuple-element.7.acc_ref, bf16[2048,256]{1,0:T(8,128)(2,1)S(1)} %copy-done), custom_call_target="tpu_custom_call" | custom-call | tf_op jit(solution)/shard_map/scatter/pallas_call | solution.py:364
Async XLA Ops:
  0.6 29.2 %copy-start = (bf16[2048,256]{1,0:T(8,128)(2,1)S(1)}, bf16[2048,256]{1,0:T(8,128)(2,1)}, u32[]{:S(2)}) copy-start(bf16[2048,256]{1,0:T(8,128)(2,1)} %table_ref.1) | copy-start | bytes 3145732
  0.6 29.2 %copy-start.1 = (s32[128]{0:T(128)S(1)}, s32[128]{0:T(128)}, u32[]{:S(2)}) copy-start(s32[128]{0:T(128)} %param.17) | copy-start | bytes 1540

commit v3 on v2

v3 whole, which is shorter than its diff:
```python
import functools

import jax
import jax.numpy as jnp
from jax import lax
from jax.experimental import pallas as pl
from jax.experimental.pallas import tpu as pltpu
from jax.sharding import PartitionSpec as P

MESH = pl.DeviceIdType.MESH
F32 = jnp.float32
BF16 = jnp.bfloat16
learn_rate = 1.0

N_CORE = 2
N_XHI = 2
N_XLO = 2
REACH = 4
UP = REACH
DOWN = REACH - 1


def split3(values):
    high = values.astype(BF16)
    rest = values - high.astype(F32)
    mid = rest.astype(BF16)
    low = (rest - mid.astype(F32)).astype(BF16)
    return high, mid, low


def dot_nn(a, b):
    return jnp.dot(a, b, preferred_element_type=F32)


def dot_nt(a, b):
    return lax.dot_general(a, b, (((1,), (1,)), ((), ())), preferred_element_type=F32)


def silu_slope(values, sigma_val):
    return sigma_val * (1.0 + values * (1.0 - sigma_val))


def iota(shape, dim):
    return lax.broadcasted_iota(jnp.int32, shape, dim)


def ring(size, shift):
    return min(shift % size, -shift % size)


def reduce_kernel(
    n_y,
    n_z,
    owner_hbm,
    slot_hbm,
    len_hbm,
    label_hbm,
    table_hbm,
    acc_hbm,
    touched_hbm,
    w_in_hbm,
    w_mid_hbm,
    gain_hbm,
    w_out_hbm,
    rows_ref,
    acc_out_ref,
    place_ref,
    rest_ref,
    owner_v,
    slot_v,
    len_s,
    label_v,
    table_v,
    acc_v,
    touched_v,
    w_in_v,
    w_mid_v,
    gain_v,
    w_out_v,
    in_sem,
    hist,
    far_recv,
    near_send,
    near_recv,
    plane_send,
    plane_recv,
    far_sems,
    far_sent,
    near_sem,
    plane_sem,
):
    rep = lax.axis_index("replica")
    mp = lax.axis_index("mp")
    core = lax.rem(mp, N_CORE)
    x_hi = lax.rem(lax.div(mp, N_CORE), N_XHI)
    z = lax.div(mp, N_CORE * N_XHI)
    y = lax.div(rep, N_XLO)
    n_x = N_XHI * N_XLO
    x = x_hi * N_XLO + lax.rem(rep, N_XLO)

    def column_peer(shift):
        z_i = lax.rem(z + (shift + n_z), n_z)
        return (rep, (z_i * N_XHI + x_hi) * N_CORE + core)

    def block(shift):
        return lax.rem(z + (shift + 2 * n_z), n_z)

    plane = [
        (dy, dx, dc)
        for dy in range(n_y)
        for dx in range(n_x)
        for dc in range(N_CORE)
        if (dy, dx, dc) != (0, 0, 0)
    ]
    plane.sort(key=lambda d: -(ring(n_y, d[0]) + ring(n_x, d[1])))
    plane_peers = []
    for dy, dx, dc in plane:
        y_i, x_i = lax.rem(y + dy, n_y), lax.rem(x + dx, n_x)
        core_i = lax.rem(core + dc, N_CORE)
        xhi_i = lax.div(x_i, N_XLO)
        rep_i = y_i * N_XLO + lax.rem(x_i, N_XLO)
        kind_i = xhi_i * N_CORE + core_i
        plane_peers.append((kind_i, (rep_i, z * (N_XHI * N_CORE) + kind_i)))
    shifts = [s for k in range(REACH, 0, -1) for s in (k, -k)]

    sources = [
        (owner_hbm, owner_v),
        (slot_hbm, slot_v),
        (label_hbm, label_v),
        (len_hbm, len_s),
        (touched_hbm, touched_v),
        (table_hbm, table_v),
        (w_in_hbm, w_in_v),
        (w_mid_hbm, w_mid_v),
        (gain_hbm, gain_v),
        (w_out_hbm, w_out_v),
        (acc_hbm, acc_v),
    ]
    loads = [
        pltpu.make_async_copy(src, dst, in_sem.at[i]) for i, (src, dst) in enumerate(sources)
    ]
    for load in loads[:4]:
        load.start()
    barrier = pltpu.get_barrier_semaphore()
    for shift in shifts:
        pl.semaphore_signal(
            barrier, inc=1, device_id=column_peer(shift), device_id_type=MESH
        )
    for _, peer in plane_peers:
        pl.semaphore_signal(barrier, inc=1, device_id=peer, device_id_type=MESH)
    for load in loads[4:]:
        load.start()

    samples, length = owner_v.shape
    n_rows = n_z * 8
    slots_n = hist.shape[2]
    row = iota((n_rows, slots_n), 0)
    counts = lax.rem(row, 2) == 0
    row_owner = lax.div(row, 2)
    slot_iota = iota((slots_n, slots_n), 0)
    lane = iota((1, slots_n), 1)
    for load in loads[:4]:
        load.wait()
    parts, hots = [[], [], []], []
    for sample in range(samples):
        for start in range(0, length, slots_n):
            window = (slice(sample, sample + 1), slice(start, start + slots_n))
            live = (lane + start < len_s[sample]).astype(F32)
            high, mid, low = (live * part.astype(F32) for part in split3(label_v[window]))
            hit = row_owner == owner_v[window]
            labelled = hit & ~counts
            parts[0].append(jnp.where(hit, jnp.where(counts, live, high), 0.0).astype(BF16))
            parts[1].append(jnp.where(labelled, mid, 0.0).astype(BF16))
            parts[2].append(jnp.where(labelled, low, 0.0).astype(BF16))
            hots.append((slot_iota == slot_v[window]).astype(F32).astype(BF16))
    stacked = jnp.concatenate([jnp.concatenate(part, axis=1) for part in parts], axis=0)
    counted = dot_nt(stacked, jnp.concatenate(hots, axis=1))
    counted = counted[:n_rows] + counted[n_rows : 2 * n_rows] + counted[2 * n_rows :]
    hist[...] = counted.reshape(n_z, 8, slots_n)

    pl.semaphore_wait(barrier, len(shifts) + len(plane_peers))

    def far(k):
        slot = k - 1 if k > 0 else UP - k - 1
        hop = REACH if k > 0 else -REACH
        return pltpu.make_async_remote_copy(
            src_ref=hist.at[block(hop + k)],
            dst_ref=far_recv.at[slot],
            send_sem=far_sent,
            recv_sem=far_sems.at[slot],
            device_id=column_peer(hop),
            device_id_type=MESH,
        )

    order = [s for s in shifts if s != -REACH]
    for k in order:
        far(k).start()

    def near(k, src):
        slot = k - 1 if k > 0 else UP - k - 1
        return pltpu.make_async_remote_copy(
            src_ref=src,
            dst_ref=near_recv.at[slot],
            send_sem=near_sem.at[0],
            recv_sem=near_sem.at[1],
            device_id=column_peer(k),
            device_id_type=MESH,
        )

    near(-REACH, hist.at[block(-REACH)]).start()
    for k in order:
        slot = k - 1 if k > 0 else UP - k - 1
        pltpu.make_async_copy(far_recv.at[slot], far_recv.at[slot], far_sems.at[slot]).wait()
        near_send[slot] = hist[block(k)] + far_recv[slot]
        near(k, near_send.at[slot]).start()

    for load in loads[4:]:
        load.wait()
    rows_n = table_v.shape[0]
    lanes = acc_v.shape[1]
    touched_row = touched_v[...]
    eye = iota((slots_n, slots_n), 0) == iota((slots_n, slots_n), 1)

    def to_column(line):
        return jnp.sum(jnp.where(eye, line, 0.0), axis=1, keepdims=True)

    touched_col = to_column(touched_row.astype(F32)).astype(jnp.int32)
    pick = (iota((slots_n, rows_n), 1) == touched_col).astype(F32).astype(BF16)
    old_rows = dot_nn(pick, table_v[...])
    gain = gain_v[...]
    w_out = w_out_v[...]
    width = w_out.shape[1]
    pre_act = dot_nn(old_rows.astype(BF16), w_in_v[...])
    sig_pre = jax.nn.sigmoid(pre_act)
    hidden = pre_act * sig_pre
    inv_rms = lax.rsqrt(jnp.sum(hidden * hidden, axis=1, keepdims=True) * (1.0 / width) + 1e-06)
    mixed = dot_nn((hidden * inv_rms * gain).astype(BF16), w_mid_v[...])
    sig_mix = jax.nn.sigmoid(mixed)
    logits = jnp.sum((hidden + mixed * sig_mix) * w_out, axis=1, keepdims=True)
    click = jax.nn.sigmoid(logits)
    d_mixed = (w_out * silu_slope(mixed, sig_mix)).astype(BF16)

    pltpu.make_async_copy(near_recv, near_recv, near_sem.at[1]).wait()
    column = hist[z]
    for slot in range(UP + REACH):
        column = column + near_recv[slot]
    n_kind = N_XHI * N_CORE
    for kind in range(n_kind):
        plane_send[kind] = column[kind * 2 : kind * 2 + 2, :]
    own_kind = x_hi * N_CORE + core
    mine = rep * n_kind + own_kind
    for kind_i, peer in plane_peers:
        pltpu.make_async_remote_copy(
            src_ref=plane_send.at[kind_i],
            dst_ref=plane_recv.at[mine],
            send_sem=plane_sem.at[0],
            recv_sem=plane_sem.at[1],
            device_id=peer,
            device_id_type=MESH,
        ).start()
    plane_recv[mine] = plane_send[own_kind]

    gained = dot_nt(d_mixed, w_mid_v[...]) * gain
    dotted = jnp.sum(hidden * gained, axis=1, keepdims=True) * (1.0 / width)
    d_hidden = w_out + inv_rms * gained - hidden * (inv_rms * inv_rms * inv_rms * dotted)
    d_pre = (d_hidden * silu_slope(pre_act, sig_pre)).astype(BF16)
    unit_grad = dot_nt(d_pre, w_in_v[...])

    lo_col = lax.rem(touched_col, lanes)
    hi_col = lax.div(touched_col, lanes)
    acc_rows = acc_v.shape[0]
    hi_hot = (iota((slots_n, acc_rows), 1) == hi_col).astype(F32).astype(BF16)
    lo_hit = iota((slots_n, lanes), 1) == lo_col
    acc_parts = [dot_nn(hi_hot, piece) for piece in split3(acc_v[...])]
    acc_lines = acc_parts[0] + acc_parts[1] + acc_parts[2]
    old_acc = jnp.sum(jnp.where(lo_hit, acc_lines, 0.0), axis=1, keepdims=True)
    hi_hot_t = (
        (iota((acc_rows, slots_n), 0) == lax.div(touched_row, lanes)).astype(F32).astype(BF16)
    )
    acc_hit = dot_nn(hi_hot_t, lo_hit.astype(F32).astype(BF16)) > 0.5

    place = (iota((rows_n, slots_n), 0) == touched_row).astype(F32).astype(BF16)
    place_ref[...] = place
    hits = dot_nn(place, jnp.ones((slots_n, table_v.shape[1]), BF16))
    rest_ref[...] = jnp.where(hits > 0.5, 0.0, table_v[...].astype(F32)).astype(BF16)

    n_p = len(plane_peers)
    pltpu.make_async_copy(
        plane_recv.at[pl.ds(0, n_p)], plane_recv.at[pl.ds(0, n_p)], plane_sem.at[1]
    ).wait()
    total = plane_recv[0]
    for i in range(1, n_p + 1):
        total = total + plane_recv[i]

    d_sum = to_column(total[0:1, :]) * click - to_column(total[1:2, :])
    grad = d_sum * unit_grad
    acc_new = old_acc + jnp.sum(grad * grad, axis=1, keepdims=True)
    rows_ref[...] = (old_rows - learn_rate * grad * lax.rsqrt(acc_new)).astype(BF16)
    spread = jnp.where(lo_hit, acc_new, 0.0)
    placed = [dot_nn(hi_hot_t, piece) for piece in split3(spread)]
    acc_out_ref[...] = jnp.where(acc_hit, placed[0] + placed[1] + placed[2], acc_v[...])

    pltpu.make_async_copy(far_recv, far_recv, far_sent).wait()
    pltpu.make_async_copy(near_recv, near_recv, near_sem.at[0]).wait()
    pltpu.make_async_copy(
        plane_recv.at[pl.ds(0, n_p)], plane_recv.at[pl.ds(0, n_p)], plane_sem.at[0]
    ).wait()


def scatter_kernel(rows_ref, acc_ref, place_ref, rest_ref, table_out, acc_out, tiles, sem):
    acc_copy = pltpu.make_async_copy(acc_ref, acc_out, sem.at[0])
    acc_copy.start()
    rows = rows_ref[...]
    count = tiles.shape[0]
    step = tiles.shape[1]
    copies = []
    for i in range(count):
        span = slice(i * step, (i + 1) * step)
        tiles[i] = (dot_nn(place_ref[span, :], rows) + rest_ref[span, :].astype(F32)).astype(BF16)
        copy = pltpu.make_async_copy(tiles.at[i], table_out.at[pl.ds(i * step, step)], sem.at[i + 1])
        copy.start()
        copies.append(copy)
    for copy in copies:
        copy.wait()
    acc_copy.wait()


def on_device(
    n_y,
    n_z,
    owner_shard,
    slot_index,
    lengths,
    labels,
    embed_table,
    accumulator,
    touched,
    w_in,
    w_mid,
    norm_gain,
    w_out,
):
    rows_n, emb = embed_table.shape
    slots_n = touched.shape[0]
    width = w_out.shape[0]
    lanes = 128
    acc2 = accumulator.reshape(rows_n // lanes, lanes)
    touched2 = touched.reshape(1, slots_n)
    hbm_spec = pl.BlockSpec(memory_space=pltpu.HBM)
    vmem = pl.BlockSpec(memory_space=pltpu.VMEM)
    n_far = UP + DOWN
    n_near = UP + REACH
    n_kind = N_XHI * N_CORE
    operands = [
        pltpu.with_memory_space_constraint(array, pltpu.HBM)
        for array in (
            owner_shard,
            slot_index,
            lengths,
            labels,
            embed_table,
            acc2,
            touched2,
            w_in,
            w_mid,
            norm_gain.reshape(1, width),
            w_out.reshape(1, width),
        )
    ]
    made = pl.pallas_call(
        functools.partial(reduce_kernel, n_y, n_z),
        out_shape=(
            jax.ShapeDtypeStruct((slots_n, emb), BF16),
            jax.ShapeDtypeStruct(acc2.shape, F32),
            jax.ShapeDtypeStruct((rows_n, slots_n), BF16),
            jax.ShapeDtypeStruct((rows_n, emb), BF16),
        ),
        in_specs=[hbm_spec] * len(operands),
        out_specs=(vmem,) * 4,
        scratch_shapes=[
            pltpu.VMEM(owner_shard.shape, jnp.int32),
            pltpu.VMEM(slot_index.shape, jnp.int32),
            pltpu.SMEM(lengths.shape, jnp.int32),
            pltpu.VMEM(labels.shape, F32),
            pltpu.VMEM(embed_table.shape, BF16),
            pltpu.VMEM(acc2.shape, F32),
            pltpu.VMEM(touched2.shape, jnp.int32),
            pltpu.VMEM(w_in.shape, BF16),
            pltpu.VMEM(w_mid.shape, BF16),
            pltpu.VMEM((1, width), F32),
            pltpu.VMEM((1, width), F32),
            pltpu.SemaphoreType.DMA((11,)),
            pltpu.VMEM((n_z, 8, slots_n), F32),
            pltpu.VMEM((n_far, 8, slots_n), F32),
            pltpu.VMEM((n_far, 8, slots_n), F32),
            pltpu.VMEM((n_near, 8, slots_n), F32),
            pltpu.VMEM((n_kind, 2, slots_n), F32),
            pltpu.VMEM((n_kind * n_y * N_XLO, 2, slots_n), F32),
            pltpu.SemaphoreType.DMA((n_far,)),
            pltpu.SemaphoreType.DMA,
            pltpu.SemaphoreType.DMA((2,)),
            pltpu.SemaphoreType.DMA((2,)),
        ],
        compiler_params=pltpu.CompilerParams(
            collective_id=0, has_side_effects=True, vmem_limit_bytes=32 * 1024 * 1024
        ),
        name="reduce",
    )(*operands)
    tiles = 4
    table_out, accum_out = pl.pallas_call(
        scatter_kernel,
        out_shape=(
            jax.ShapeDtypeStruct(embed_table.shape, BF16),
            jax.ShapeDtypeStruct(acc2.shape, F32),
        ),
        in_specs=[vmem] * 4,
        out_specs=(hbm_spec,) * 2,
        scratch_shapes=[
            pltpu.VMEM((tiles, rows_n // tiles, emb), BF16),
            pltpu.SemaphoreType.DMA((tiles + 1,)),
        ],
        compiler_params=pltpu.CompilerParams(vmem_limit_bytes=24 * 1024 * 1024),
        name="scatter",
    )(*made)
    return (table_out, accum_out.reshape(rows_n))


def solution(mesh):
    n_y = mesh.shape["replica"] // N_XLO
    n_z = mesh.shape["mp"] // (N_CORE * N_XHI)
    in_specs = (
        P(("replica", "mp"), None),
        P(("replica", "mp"), None),
        P(("replica", "mp")),
        P(("replica", "mp"), None),
        P("mp", None),
        P("mp"),
        P("mp"),
        P(),
        P(),
        P(),
        P(),
    )
    out_specs = (P("mp", None), P("mp"))
    return jax.shard_map(
        functools.partial(on_device, n_y, n_z),
        mesh=mesh,
        in_specs=in_specs,
        out_specs=out_specs,
        check_vma=False,
    )
```

time: 31.5 us -> 31.7 us (level)
    pallas_call x1, Pallas kernels: 29.2 us -> 29.6 us  [on_device(): pl.pallas_call(functools.partial(reduce_kernel, n_y, n_z), out_shape=(jax...]
where the time goes in v3:
time: 31.7 us; the launch traced here: 31.5 us
  Pallas kernels  30.9 us (97%)
  between operations  0.64 us (2%)
    pallas_call x1, Pallas kernels, on_device(): pl.pallas_call(functools.partial(reduce_kernel, n_y, n_z), out_shape=(jax...  29.6 us
    pallas_call x1, Pallas kernels, on_device(): pl.pallas_call(scatter_kernel, out_shape=(jax.ShapeDtypeStruct(embed_tabl...  1.29 us

profile of v3, /device:TPU:1, one launch (start us, length us, event | category | flops | bytes accessed | tf_op | source)
XLA Modules:
  0.0 31.5 jit_solution(17436671688833032088)
XLA Ops:
  0.6 29.6 %reduce.1 = (bf16[128,256]{1,0:T(8,128)(2,1)S(1)}, f32[16,128]{1,0:T(8,128)S(1)}, bf16[2048,128]{1,0:T(8,128)(2,1)S(1)}, bf16[2048,256]{1,0:T(8,128)(2,1)S(1)}) custom-call(s32[2,256]{1,0:T(2,128)} %owner_hbm.1, s32[2,256]{1,0:T(2,128)} %slot_hbm.1, s32[2]{0:T(128)} %len_hbm.1, f32[2,256]{1,0:T(2,128)} %label_hbm.1, bf16[2048,256]{1,0:T(8,128)(2,1)} %table_hbm.1, ...), custom_call_target="tpu_custom_call" | custom-call | tf_op jit(solution)/shard_map/reduce/pallas_call | solution.py:370
  30.2 1.3 %scatter.1 = (bf16[2048,256]{1,0:T(8,128)(2,1)}, f32[16,128]{1,0:T(8,128)}) custom-call(bf16[128,256]{1,0:T(8,128)(2,1)S(1)} %get-tuple-element.8.rows_ref, f32[16,128]{1,0:T(8,128)S(1)} %get-tuple-element.9.acc_ref, bf16[2048,128]{1,0:T(8,128)(2,1)S(1)} %get-tuple-element.10.place_ref, bf16[2048,256]{1,0:T(8,128)(2,1)S(1)} %get-tuple-element.11.rest_ref), custom_call_target="tpu_custom_call" | custom-call | tf_op jit(solution)/shard_map/scatter/pallas_call | solution.py:410

commit v4 on v3

--- a/solution.py
+++ b/solution.py
@@ -82,11 +82,13 @@
     far_recv,
     near_send,
     near_recv,
+    core_recv,
     plane_send,
     plane_recv,
     far_sems,
     far_sent,
     near_sem,
+    core_sem,
     plane_sem,
 ):
     rep = lax.axis_index("replica")
@@ -98,29 +100,22 @@
     n_x = N_XHI * N_XLO
     x = x_hi * N_XLO + lax.rem(rep, N_XLO)
 
-    def column_peer(shift):
+    def column_peer(shift, turn=0):
         z_i = lax.rem(z + (shift + n_z), n_z)
-        return (rep, (z_i * N_XHI + x_hi) * N_CORE + core)
+        return (rep, (z_i * N_XHI + x_hi) * N_CORE + lax.rem(core + turn, N_CORE))
 
     def block(shift):
         return lax.rem(z + (shift + 2 * n_z), n_z)
 
-    plane = [
-        (dy, dx, dc)
-        for dy in range(n_y)
-        for dx in range(n_x)
-        for dc in range(N_CORE)
-        if (dy, dx, dc) != (0, 0, 0)
-    ]
+    plane = [(dy, dx) for dy in range(n_y) for dx in range(n_x) if (dy, dx) != (0, 0)]
     plane.sort(key=lambda d: -(ring(n_y, d[0]) + ring(n_x, d[1])))
     plane_peers = []
-    for dy, dx, dc in plane:
+    for dy, dx in plane:
         y_i, x_i = lax.rem(y + dy, n_y), lax.rem(x + dx, n_x)
-        core_i = lax.rem(core + dc, N_CORE)
         xhi_i = lax.div(x_i, N_XLO)
         rep_i = y_i * N_XLO + lax.rem(x_i, N_XLO)
-        kind_i = xhi_i * N_CORE + core_i
-        plane_peers.append((kind_i, (rep_i, z * (N_XHI * N_CORE) + kind_i)))
+        plane_peers.append((xhi_i, (rep_i, (z * N_XHI + xhi_i) * N_CORE + core)))
+    partner = (rep, mp + 1 - 2 * core)
     shifts = [s for k in range(REACH, 0, -1) for s in (k, -k)]
 
     sources = [
@@ -139,24 +134,28 @@
     loads = [
         pltpu.make_async_copy(src, dst, in_sem.at[i]) for i, (src, dst) in enumerate(sources)
     ]
-    for load in loads[:4]:
-        load.start()
     barrier = pltpu.get_barrier_semaphore()
     for shift in shifts:
         pl.semaphore_signal(
             barrier, inc=1, device_id=column_peer(shift), device_id_type=MESH
         )
-    for _, peer in plane_peers:
+    for load in loads[:4]:
+        load.start()
+    others = [column_peer(REACH, 1), column_peer(-REACH, 1), partner]
+    for peer in others + [peer for _, peer in plane_peers]:
         pl.semaphore_signal(barrier, inc=1, device_id=peer, device_id_type=MESH)
     for load in loads[4:]:
         load.start()
 
     samples, length = owner_v.shape
-    n_rows = n_z * 8
+    part = hist.shape[1]
+    n_rows = hist.shape[0] * part
     slots_n = hist.shape[2]
     row = iota((n_rows, slots_n), 0)
     counts = lax.rem(row, 2) == 0
-    row_owner = lax.div(row, 2)
+    row_z = lax.rem(lax.div(row, part), n_z)
+    row_x = lax.rem(lax.div(row, 2), N_XHI)
+    row_owner = (row_z * N_XHI + row_x) * N_CORE + lax.div(row, n_z * part)
     slot_iota = iota((slots_n, slots_n), 0)
     lane = iota((1, slots_n), 1)
     for load in loads[:4]:
@@ -176,43 +175,58 @@
     stacked = jnp.concatenate([jnp.concatenate(part, axis=1) for part in parts], axis=0)
     counted = dot_nt(stacked, jnp.concatenate(hots, axis=1))
     counted = counted[:n_rows] + counted[n_rows : 2 * n_rows] + counted[2 * n_rows :]
-    hist[...] = counted.reshape(n_z, 8, slots_n)
-
-    pl.semaphore_wait(barrier, len(shifts) + len(plane_peers))
-
-    def far(k):
-        slot = k - 1 if k > 0 else UP - k - 1
-        hop = REACH if k > 0 else -REACH
-        return pltpu.make_async_remote_copy(
-            src_ref=hist.at[block(hop + k)],
-            dst_ref=far_recv.at[slot],
-            send_sem=far_sent,
-            recv_sem=far_sems.at[slot],
-            device_id=column_peer(hop),
-            device_id_type=MESH,
-        )
+    for i in range(N_CORE * n_z):
+        hist[i] = counted[i * part : (i + 1) * part, :]
+
+    pl.semaphore_wait(barrier, len(shifts) + len(plane_peers) + len(others))
+
+    core_copy = pltpu.make_async_remote_copy(
+        src_ref=hist.at[pl.ds((1 - core) * n_z, n_z)],
+        dst_ref=core_recv,
+        send_sem=core_sem.at[0],
+        recv_sem=core_sem.at[1],
+        device_id=partner,
+        device_id_type=MESH,
+    )
+    core_copy.start()
+
+    def slot_of(k):
+        return k - 1 if k > 0 else UP - k - 1
 
     order = [s for s in shifts if s != -REACH]
     for k in order:
-        far(k).start()
-
-    def near(k, src):
-        slot = k - 1 if k > 0 else UP - k - 1
-        return pltpu.make_async_remote_copy(
-            src_ref=src,
+        hop = REACH if k > 0 else -REACH
+        for turn in (1, 0):
+            pltpu.make_async_remote_copy(
+                src_ref=hist.at[lax.rem(core + turn, N_CORE) * n_z + block(hop + k)],
+                dst_ref=far_recv.at[slot_of(k), core],
+                send_sem=far_sent,
+                recv_sem=far_sems.at[slot_of(k)],
+                device_id=column_peer(hop, turn),
+                device_id_type=MESH,
+            ).start()
+
+    core_copy.wait_recv()
+
+    def both(z_i):
+        return hist[core * n_z + z_i] + core_recv[z_i]
+
+    for k in [-REACH] + order:
+        slot = slot_of(k)
+        own = both(block(k))
+        if k != -REACH:
+            arrived = far_recv.at[slot]
+            pltpu.make_async_copy(arrived, arrived, far_sems.at[slot]).wait()
+            own = own + (far_recv[slot, 0] + far_recv[slot, 1])
+        near_send[slot] = own
+        pltpu.make_async_remote_copy(
+            src_ref=near_send.at[slot],
             dst_ref=near_recv.at[slot],
             send_sem=near_sem.at[0],
             recv_sem=near_sem.at[1],
             device_id=column_peer(k),
             device_id_type=MESH,
-        )
-
-    near(-REACH, hist.at[block(-REACH)]).start()
-    for k in order:
-        slot = k - 1 if k > 0 else UP - k - 1
-        pltpu.make_async_copy(far_recv.at[slot], far_recv.at[slot], far_sems.at[slot]).wait()
-        near_send[slot] = hist[block(k)] + far_recv[slot]
-        near(k, near_send.at[slot]).start()
+        ).start()
 
     for load in loads[4:]:
         load.wait()
@@ -241,24 +255,22 @@
     d_mixed = (w_out * silu_slope(mixed, sig_mix)).astype(BF16)
 
     pltpu.make_async_copy(near_recv, near_recv, near_sem.at[1]).wait()
-    column = hist[z]
+    column = both(z)
     for slot in range(UP + REACH):
         column = column + near_recv[slot]
-    n_kind = N_XHI * N_CORE
-    for kind in range(n_kind):
-        plane_send[kind] = column[kind * 2 : kind * 2 + 2, :]
-    own_kind = x_hi * N_CORE + core
-    mine = rep * n_kind + own_kind
-    for kind_i, peer in plane_peers:
+    for x_i in range(N_XHI):
+        plane_send[x_i] = column[x_i * 2 : x_i * 2 + 2, :]
+    mine = rep * N_XHI + x_hi
+    for xhi_i, peer in plane_peers:
         pltpu.make_async_remote_copy(
-            src_ref=plane_send.at[kind_i],
+            src_ref=plane_send.at[xhi_i],
             dst_ref=plane_recv.at[mine],
             send_sem=plane_sem.at[0],
             recv_sem=plane_sem.at[1],
             device_id=peer,
             device_id_type=MESH,
         ).start()
-    plane_recv[mine] = plane_send[own_kind]
+    plane_recv[mine] = plane_send[x_hi]
 
     gained = dot_nt(d_mixed, w_mid_v[...]) * gain
     dotted = jnp.sum(hidden * gained, axis=1, keepdims=True) * (1.0 / width)
@@ -300,6 +312,7 @@
     placed = [dot_nn(hi_hot_t, piece) for piece in split3(spread)]
     acc_out_ref[...] = jnp.where(acc_hit, placed[0] + placed[1] + placed[2], acc_v[...])
 
+    core_copy.wait_send()
     pltpu.make_async_copy(far_recv, far_recv, far_sent).wait()
     pltpu.make_async_copy(near_recv, near_recv, near_sem.at[0]).wait()
     pltpu.make_async_copy(
@@ -350,7 +363,7 @@
     vmem = pl.BlockSpec(memory_space=pltpu.VMEM)
     n_far = UP + DOWN
     n_near = UP + REACH
-    n_kind = N_XHI * N_CORE
+    part = N_XHI * 2
     operands = [
         pltpu.with_memory_space_constraint(array, pltpu.HBM)
         for array in (
@@ -390,14 +403,16 @@
             pltpu.VMEM((1, width), F32),
             pltpu.VMEM((1, width), F32),
             pltpu.SemaphoreType.DMA((11,)),
-            pltpu.VMEM((n_z, 8, slots_n), F32),
-            pltpu.VMEM((n_far, 8, slots_n), F32),
-            pltpu.VMEM((n_far, 8, slots_n), F32),
-            pltpu.VMEM((n_near, 8, slots_n), F32),
-            pltpu.VMEM((n_kind, 2, slots_n), F32),
-            pltpu.VMEM((n_kind * n_y * N_XLO, 2, slots_n), F32),
+            pltpu.VMEM((N_CORE * n_z, part, slots_n), F32),
+            pltpu.VMEM((n_far, N_CORE, part, slots_n), F32),
+            pltpu.VMEM((n_near, part, slots_n), F32),
+            pltpu.VMEM((n_near, part, slots_n), F32),
+            pltpu.VMEM((n_z, part, slots_n), F32),
+            pltpu.VMEM((N_XHI, 2, slots_n), F32),
+            pltpu.VMEM((N_XHI * n_y * N_XLO, 2, slots_n), F32),
             pltpu.SemaphoreType.DMA((n_far,)),
             pltpu.SemaphoreType.DMA,
+            pltpu.SemaphoreType.DMA((2,)),
             pltpu.SemaphoreType.DMA((2,)),
             pltpu.SemaphoreType.DMA((2,)),
         ],

time: 31.7 us -> 29.9 us (0.943)
  Pallas kernels: 30.9 us -> 29.1 us
    pallas_call x1, Pallas kernels: 29.6 us -> 27.8 us  [on_device(): pl.pallas_call(functools.partial(reduce_kernel, n_y, n_z), out_shape=(jax...]
where the time goes in v4:
time: 29.9 us; the launch traced here: 29.8 us
  Pallas kernels  29.1 us (97%)
  between operations  0.64 us (2%)
    pallas_call x1, Pallas kernels, on_device(): pl.pallas_call(functools.partial(reduce_kernel, n_y, n_z), out_shape=(jax...  27.8 us
    pallas_call x1, Pallas kernels, on_device(): pl.pallas_call(scatter_kernel, out_shape=(jax.ShapeDtypeStruct(embed_tabl...  1.29 us

profile of v4, /device:TPU:1, one launch (start us, length us, event | category | flops | bytes accessed | tf_op | source)
XLA Modules:
  0.0 29.8 jit_solution(18103168217931166575)
XLA Ops:
  0.6 27.8 %reduce.1 = (bf16[128,256]{1,0:T(8,128)(2,1)S(1)}, f32[16,128]{1,0:T(8,128)S(1)}, bf16[2048,128]{1,0:T(8,128)(2,1)S(1)}, bf16[2048,256]{1,0:T(8,128)(2,1)S(1)}) custom-call(s32[2,256]{1,0:T(2,128)} %owner_hbm.1, s32[2,256]{1,0:T(2,128)} %slot_hbm.1, s32[2]{0:T(128)} %len_hbm.1, f32[2,256]{1,0:T(2,128)} %label_hbm.1, bf16[2048,256]{1,0:T(8,128)(2,1)} %table_hbm.1, ...), custom_call_target="tpu_custom_call" | custom-call | tf_op jit(solution)/shard_map/reduce/pallas_call | solution.py:383
  28.5 1.3 %scatter.1 = (bf16[2048,256]{1,0:T(8,128)(2,1)}, f32[16,128]{1,0:T(8,128)}) custom-call(bf16[128,256]{1,0:T(8,128)(2,1)S(1)} %get-tuple-element.8.rows_ref, f32[16,128]{1,0:T(8,128)S(1)} %get-tuple-element.9.acc_ref, bf16[2048,128]{1,0:T(8,128)(2,1)S(1)} %get-tuple-element.10.place_ref, bf16[2048,256]{1,0:T(8,128)(2,1)S(1)} %get-tuple-element.11.rest_ref), custom_call_target="tpu_custom_call" | custom-call | tf_op jit(solution)/shard_map/scatter/pallas_call | solution.py:425

commit v5 on v4

--- a/solution.py
+++ b/solution.py
@@ -63,9 +63,11 @@
     gain_hbm,
     w_out_hbm,
     rows_ref,
-    acc_out_ref,
+    acc_ref,
     place_ref,
     rest_ref,
+    hi_hot_ref,
+    acc_rest_ref,
     owner_v,
     slot_v,
     len_s,
@@ -135,15 +137,16 @@
         pltpu.make_async_copy(src, dst, in_sem.at[i]) for i, (src, dst) in enumerate(sources)
     ]
     barrier = pltpu.get_barrier_semaphore()
-    for shift in shifts:
-        pl.semaphore_signal(
-            barrier, inc=1, device_id=column_peer(shift), device_id_type=MESH
-        )
+    greeted = (
+        [column_peer(hop, turn) for turn in range(N_CORE) for hop in (REACH, -REACH)]
+        + [column_peer(shift) for shift in shifts if abs(shift) != REACH]
+        + [peer for _, peer in plane_peers]
+        + [partner]
+    )
+    for peer in greeted:
+        pl.semaphore_signal(barrier, inc=1, device_id=peer, device_id_type=MESH)
     for load in loads[:4]:
         load.start()
-    others = [column_peer(REACH, 1), column_peer(-REACH, 1), partner]
-    for peer in others + [peer for _, peer in plane_peers]:
-        pl.semaphore_signal(barrier, inc=1, device_id=peer, device_id_type=MESH)
     for load in loads[4:]:
         load.start()
 
@@ -178,7 +181,7 @@
     for i in range(N_CORE * n_z):
         hist[i] = counted[i * part : (i + 1) * part, :]
 
-    pl.semaphore_wait(barrier, len(shifts) + len(plane_peers) + len(others))
+    pl.semaphore_wait(barrier, len(greeted))
 
     core_copy = pltpu.make_async_remote_copy(
         src_ref=hist.at[pl.ds((1 - core) * n_z, n_z)],
@@ -277,6 +280,7 @@
     d_hidden = w_out + inv_rms * gained - hidden * (inv_rms * inv_rms * inv_rms * dotted)
     d_pre = (d_hidden * silu_slope(pre_act, sig_pre)).astype(BF16)
     unit_grad = dot_nt(d_pre, w_in_v[...])
+    unit_square = jnp.sum(unit_grad * unit_grad, axis=1, keepdims=True)
 
     lo_col = lax.rem(touched_col, lanes)
     hi_col = lax.div(touched_col, lanes)
@@ -289,7 +293,9 @@
     hi_hot_t = (
         (iota((acc_rows, slots_n), 0) == lax.div(touched_row, lanes)).astype(F32).astype(BF16)
     )
+    hi_hot_ref[...] = hi_hot_t
     acc_hit = dot_nn(hi_hot_t, lo_hit.astype(F32).astype(BF16)) > 0.5
+    acc_rest_ref[...] = jnp.where(acc_hit, 0.0, acc_v[...])
 
     place = (iota((rows_n, slots_n), 0) == touched_row).astype(F32).astype(BF16)
     place_ref[...] = place
@@ -305,12 +311,9 @@
         total = total + plane_recv[i]
 
     d_sum = to_column(total[0:1, :]) * click - to_column(total[1:2, :])
-    grad = d_sum * unit_grad
-    acc_new = old_acc + jnp.sum(grad * grad, axis=1, keepdims=True)
-    rows_ref[...] = (old_rows - learn_rate * grad * lax.rsqrt(acc_new)).astype(BF16)
-    spread = jnp.where(lo_hit, acc_new, 0.0)
-    placed = [dot_nn(hi_hot_t, piece) for piece in split3(spread)]
-    acc_out_ref[...] = jnp.where(acc_hit, placed[0] + placed[1] + placed[2], acc_v[...])
+    acc_new = old_acc + d_sum * d_sum * unit_square
+    rows_ref[...] = (old_rows - (learn_rate * d_sum * lax.rsqrt(acc_new)) * unit_grad).astype(BF16)
+    acc_ref[...] = jnp.where(lo_hit, acc_new, 0.0)
 
     core_copy.wait_send()
     pltpu.make_async_copy(far_recv, far_recv, far_sent).wait()
@@ -320,9 +323,9 @@
     ).wait()
 
 
-def scatter_kernel(rows_ref, acc_ref, place_ref, rest_ref, table_out, acc_out, tiles, sem):
-    acc_copy = pltpu.make_async_copy(acc_ref, acc_out, sem.at[0])
-    acc_copy.start()
+def scatter_kernel(
+    rows_ref, acc_ref, place_ref, rest_ref, hi_hot_ref, acc_rest_ref, table_out, acc_out, tiles, acc_tile, sem
+):
     rows = rows_ref[...]
     count = tiles.shape[0]
     step = tiles.shape[1]
@@ -330,12 +333,17 @@
     for i in range(count):
         span = slice(i * step, (i + 1) * step)
         tiles[i] = (dot_nn(place_ref[span, :], rows) + rest_ref[span, :].astype(F32)).astype(BF16)
-        copy = pltpu.make_async_copy(tiles.at[i], table_out.at[pl.ds(i * step, step)], sem.at[i + 1])
-        copy.start()
-        copies.append(copy)
+        copies.append(
+            pltpu.make_async_copy(tiles.at[i], table_out.at[pl.ds(i * step, step)], sem.at[i + 1])
+        )
+        copies[-1].start()
+        if i == count - 2:
+            placed = [dot_nn(hi_hot_ref[...], piece) for piece in split3(acc_ref[...])]
+            acc_tile[...] = acc_rest_ref[...] + (placed[0] + placed[1] + placed[2])
+            copies.append(pltpu.make_async_copy(acc_tile, acc_out, sem.at[0]))
+            copies[-1].start()
     for copy in copies:
         copy.wait()
-    acc_copy.wait()
 
 
 def on_device(
@@ -384,12 +392,14 @@
         functools.partial(reduce_kernel, n_y, n_z),
         out_shape=(
             jax.ShapeDtypeStruct((slots_n, emb), BF16),
-            jax.ShapeDtypeStruct(acc2.shape, F32),
+            jax.ShapeDtypeStruct((slots_n, lanes), F32),
             jax.ShapeDtypeStruct((rows_n, slots_n), BF16),
             jax.ShapeDtypeStruct((rows_n, emb), BF16),
+            jax.ShapeDtypeStruct((acc2.shape[0], slots_n), BF16),
+            jax.ShapeDtypeStruct(acc2.shape, F32),
         ),
         in_specs=[hbm_spec] * len(operands),
-        out_specs=(vmem,) * 4,
+        out_specs=(vmem,) * 6,
         scratch_shapes=[
             pltpu.VMEM(owner_shard.shape, jnp.int32),
             pltpu.VMEM(slot_index.shape, jnp.int32),
@@ -428,10 +438,11 @@
             jax.ShapeDtypeStruct(embed_table.shape, BF16),
             jax.ShapeDtypeStruct(acc2.shape, F32),
         ),
-        in_specs=[vmem] * 4,
+        in_specs=[vmem] * 6,
         out_specs=(hbm_spec,) * 2,
         scratch_shapes=[
             pltpu.VMEM((tiles, rows_n // tiles, emb), BF16),
+            pltpu.VMEM(acc2.shape, F32),
             pltpu.SemaphoreType.DMA((tiles + 1,)),
         ],
         compiler_params=pltpu.CompilerParams(vmem_limit_bytes=24 * 1024 * 1024),

time: 29.9 us -> 29.6 us (0.990)
  no operation moved by 1% of the time
where the time goes in v5:
time: 29.6 us; the launch traced here: 29.5 us
  Pallas kernels  28.9 us (98%)
  between operations  0.64 us (2%)
    pallas_call x1, Pallas kernels, on_device(): pl.pallas_call(functools.partial(reduce_kernel, n_y, n_z), out_shape=(jax...  27.6 us
    pallas_call x1, Pallas kernels, on_device(): pl.pallas_call(scatter_kernel, out_shape=(jax.ShapeDtypeStruct(embed_tabl...  1.3 us

profile of v5, /device:TPU:1, one launch (start us, length us, event | category | flops | bytes accessed | tf_op | source)
XLA Modules:
  0.0 29.5 jit_solution(15008980801065972488)
XLA Ops:
  0.6 27.6 %reduce.1 = (bf16[128,256]{1,0:T(8,128)(2,1)S(1)}, f32[128,128]{1,0:T(8,128)S(1)}, bf16[2048,128]{1,0:T(8,128)(2,1)S(1)}, bf16[2048,256]{1,0:T(8,128)(2,1)S(1)},...) custom-call(s32[2,256]{1,0:T(2,128)} %owner_hbm.1, s32[2,256]{1,0:T(2,128)} %slot_hbm.1, s32[2]{0:T(128)} %len_hbm.1, ...), custom_call_target="tpu_custom_call" | custom-call | tf_op jit(solution)/shard_map/reduce/pallas_call | solution.py:391
  28.2 1.3 %scatter.1 = (bf16[2048,256]{1,0:T(8,128)(2,1)}, f32[16,128]{1,0:T(8,128)}) custom-call(bf16[128,256]{1,0:T(8,128)(2,1)S(1)} %get-tuple-element.10.rows_ref, f32[128,128]{1,0:T(8,128)S(1)} %get-tuple-element.11.acc_ref, bf16[2048,128]{1,0:T(8,128)(2,1)S(1)} %get-tuple-element.12.place_ref, bf16[2048,256]{1,0:T(8,128)(2,1)S(1)} %get-tuple-element.13.rest_ref, ...), custom_call_target="tpu_custom_call" | custom-call | tf_op jit(solution)/shard_map/scatter/pallas_call | solution.py:435

commit v6 on v5

--- a/solution.py
+++ b/solution.py
@@ -34,6 +34,13 @@
 
 def dot_nt(a, b):
     return lax.dot_general(a, b, (((1,), (1,)), ((), ())), preferred_element_type=F32)
+
+
+def tree_sum(terms):
+    while len(terms) > 1:
+        pairs = [a + b for a, b in zip(terms[::2], terms[1::2])]
+        terms = pairs + terms[2 * len(pairs) :]
+    return terms[0]
 
 
 def silu_slope(values, sigma_val):
@@ -254,13 +261,11 @@
     mixed = dot_nn((hidden * inv_rms * gain).astype(BF16), w_mid_v[...])
     sig_mix = jax.nn.sigmoid(mixed)
     logits = jnp.sum((hidden + mixed * sig_mix) * w_out, axis=1, keepdims=True)
-    click = jax.nn.sigmoid(logits)
+    click_row = jnp.sum(jnp.where(eye, jax.nn.sigmoid(logits), 0.0), axis=0, keepdims=True)
     d_mixed = (w_out * silu_slope(mixed, sig_mix)).astype(BF16)
 
     pltpu.make_async_copy(near_recv, near_recv, near_sem.at[1]).wait()
-    column = both(z)
-    for slot in range(UP + REACH):
-        column = column + near_recv[slot]
+    column = tree_sum([both(z)] + [near_recv[slot] for slot in range(UP + REACH)])
     for x_i in range(N_XHI):
         plane_send[x_i] = column[x_i * 2 : x_i * 2 + 2, :]
     mine = rep * N_XHI + x_hi
@@ -306,11 +311,9 @@
     pltpu.make_async_copy(
         plane_recv.at[pl.ds(0, n_p)], plane_recv.at[pl.ds(0, n_p)], plane_sem.at[1]
     ).wait()
-    total = plane_recv[0]
-    for i in range(1, n_p + 1):
-        total = total + plane_recv[i]
-
-    d_sum = to_column(total[0:1, :]) * click - to_column(total[1:2, :])
+    total = tree_sum([plane_recv[i] for i in range(n_p + 1)])
+
+    d_sum = to_column(total[0:1, :] * click_row - total[1:2, :])
     acc_new = old_acc + d_sum * d_sum * unit_square
     rows_ref[...] = (old_rows - (learn_rate * d_sum * lax.rsqrt(acc_new)) * unit_grad).astype(BF16)
     acc_ref[...] = jnp.where(lo_hit, acc_new, 0.0)

time: 29.6 us -> 29.6 us (level)
  no operation moved by 1% of the time
where the time goes in v6:
time: 29.6 us; the launch traced here: 29.5 us
  Pallas kernels  28.8 us (97%)
  between operations  0.64 us (2%)
    pallas_call x1, Pallas kernels, on_device(): pl.pallas_call(functools.partial(reduce_kernel, n_y, n_z), out_shape=(jax...  27.5 us
    pallas_call x1, Pallas kernels, on_device(): pl.pallas_call(scatter_kernel, out_shape=(jax.ShapeDtypeStruct(embed_tabl...  1.31 us

profile of v6, /device:TPU:1, one launch (start us, length us, event | category | flops | bytes accessed | tf_op | source)
XLA Modules:
  0.0 29.5 jit_solution(11781083992989502924)
XLA Ops:
  0.6 27.5 %reduce.1 = (bf16[128,256]{1,0:T(8,128)(2,1)S(1)}, f32[128,128]{1,0:T(8,128)S(1)}, bf16[2048,128]{1,0:T(8,128)(2,1)S(1)}, bf16[2048,256]{1,0:T(8,128)(2,1)S(1)},...) custom-call(s32[2,256]{1,0:T(2,128)} %owner_hbm.1, s32[2,256]{1,0:T(2,128)} %slot_hbm.1, s32[2]{0:T(128)} %len_hbm.1, ...), custom_call_target="tpu_custom_call" | custom-call | tf_op jit(solution)/shard_map/reduce/pallas_call | solution.py:394
  28.2 1.3 %scatter.1 = (bf16[2048,256]{1,0:T(8,128)(2,1)}, f32[16,128]{1,0:T(8,128)}) custom-call(bf16[128,256]{1,0:T(8,128)(2,1)S(1)} %get-tuple-element.10.rows_ref, f32[128,128]{1,0:T(8,128)S(1)} %get-tuple-element.11.acc_ref, bf16[2048,128]{1,0:T(8,128)(2,1)S(1)} %get-tuple-element.12.place_ref, bf16[2048,256]{1,0:T(8,128)(2,1)S(1)} %get-tuple-element.13.rest_ref, ...), custom_call_target="tpu_custom_call" | custom-call | tf_op jit(solution)/shard_map/scatter/pallas_call | solution.py:438

commit v7 on v6

--- a/solution.py
+++ b/solution.py
@@ -340,7 +340,7 @@
             pltpu.make_async_copy(tiles.at[i], table_out.at[pl.ds(i * step, step)], sem.at[i + 1])
         )
         copies[-1].start()
-        if i == count - 2:
+        if i == count - 1:
             placed = [dot_nn(hi_hot_ref[...], piece) for piece in split3(acc_ref[...])]
             acc_tile[...] = acc_rest_ref[...] + (placed[0] + placed[1] + placed[2])
             copies.append(pltpu.make_async_copy(acc_tile, acc_out, sem.at[0]))

time: 29.6 us -> 29.6 us (level)
  no operation moved by 1% of the time
where the time goes in v7:
time: 29.6 us; the launch traced here: 29.5 us
  Pallas kernels  28.8 us (97%)
  between operations  0.64 us (2%)
    pallas_call x1, Pallas kernels, on_device(): pl.pallas_call(functools.partial(reduce_kernel, n_y, n_z), out_shape=(jax...  27.5 us
    pallas_call x1, Pallas kernels, on_device(): pl.pallas_call(scatter_kernel, out_shape=(jax.ShapeDtypeStruct(embed_tabl...  1.29 us

profile of v7, /device:TPU:1, one launch (start us, length us, event | category | flops | bytes accessed | tf_op | source)
XLA Modules:
  0.0 29.5 jit_solution(16480591032125779672)
XLA Ops:
  0.6 27.5 %reduce.1 = (bf16[128,256]{1,0:T(8,128)(2,1)S(1)}, f32[128,128]{1,0:T(8,128)S(1)}, bf16[2048,128]{1,0:T(8,128)(2,1)S(1)}, bf16[2048,256]{1,0:T(8,128)(2,1)S(1)},...) custom-call(s32[2,256]{1,0:T(2,128)} %owner_hbm.1, s32[2,256]{1,0:T(2,128)} %slot_hbm.1, s32[2]{0:T(128)} %len_hbm.1, ...), custom_call_target="tpu_custom_call" | custom-call | tf_op jit(solution)/shard_map/reduce/pallas_call | solution.py:394
  28.2 1.3 %scatter.1 = (bf16[2048,256]{1,0:T(8,128)(2,1)}, f32[16,128]{1,0:T(8,128)}) custom-call(bf16[128,256]{1,0:T(8,128)(2,1)S(1)} %get-tuple-element.10.rows_ref, f32[128,128]{1,0:T(8,128)S(1)} %get-tuple-element.11.acc_ref, bf16[2048,128]{1,0:T(8,128)(2,1)S(1)} %get-tuple-element.12.place_ref, bf16[2048,256]{1,0:T(8,128)(2,1)S(1)} %get-tuple-element.13.rest_ref, ...), custom_call_target="tpu_custom_call" | custom-call | tf_op jit(solution)/shard_map/scatter/pallas_call | solution.py:438

commit v8 on v7

--- a/solution.py
+++ b/solution.py
@@ -198,7 +198,6 @@
         device_id=partner,
         device_id_type=MESH,
     )
-    core_copy.start()
 
     def slot_of(k):
         return k - 1 if k > 0 else UP - k - 1
@@ -215,6 +214,8 @@
                 device_id=column_peer(hop, turn),
                 device_id_type=MESH,
             ).start()
+
+    core_copy.start()
 
     core_copy.wait_recv()
 

time: 29.6 us -> 29.6 us (level)
  no operation moved by 1% of the time
where the time goes in v8:
time: 29.6 us; the launch traced here: 29.5 us
  Pallas kernels  28.8 us (97%)
  between operations  0.64 us (2%)
    pallas_call x1, Pallas kernels, on_device(): pl.pallas_call(functools.partial(reduce_kernel, n_y, n_z), out_shape=(jax...  27.5 us
    pallas_call x1, Pallas kernels, on_device(): pl.pallas_call(scatter_kernel, out_shape=(jax.ShapeDtypeStruct(embed_tabl...  1.29 us

profile of v8, /device:TPU:1, one launch (start us, length us, event | category | flops | bytes accessed | tf_op | source)
XLA Modules:
  0.0 29.5 jit_solution(8926376044926683018)
XLA Ops:
  0.6 27.5 %reduce.1 = (bf16[128,256]{1,0:T(8,128)(2,1)S(1)}, f32[128,128]{1,0:T(8,128)S(1)}, bf16[2048,128]{1,0:T(8,128)(2,1)S(1)}, bf16[2048,256]{1,0:T(8,128)(2,1)S(1)},...) custom-call(s32[2,256]{1,0:T(2,128)} %owner_hbm.1, s32[2,256]{1,0:T(2,128)} %slot_hbm.1, s32[2]{0:T(128)} %len_hbm.1, ...), custom_call_target="tpu_custom_call" | custom-call | tf_op jit(solution)/shard_map/reduce/pallas_call | solution.py:395
  28.2 1.3 %scatter.1 = (bf16[2048,256]{1,0:T(8,128)(2,1)}, f32[16,128]{1,0:T(8,128)}) custom-call(bf16[128,256]{1,0:T(8,128)(2,1)S(1)} %get-tuple-element.10.rows_ref, f32[128,128]{1,0:T(8,128)S(1)} %get-tuple-element.11.acc_ref, bf16[2048,128]{1,0:T(8,128)(2,1)S(1)} %get-tuple-element.12.place_ref, bf16[2048,256]{1,0:T(8,128)(2,1)S(1)} %get-tuple-element.13.rest_ref, ...), custom_call_target="tpu_custom_call" | custom-call | tf_op jit(solution)/shard_map/scatter/pallas_call | solution.py:439
